TPU v7x, 32 devices: a whole 2x2x4 slice. The times are simulated.
32 devices in a mesh: row: 8 (over y, x, core), col: 4 (over z).
Axes of the slice: x: 2, y: 2, z: 4, core: 2. Of those that a mesh axis runs over, the one named last changes fastest.
Arguments:
- integrals: bfloat16 [3072, 192], P('row', 'col'), may hold values from -0.4375 to 0.4375
- amplitudes: bfloat16 [192, 3072], P('row', 'col'), may hold values from -6 to 6
- energies: float32 [3072], replicated, may hold values from 0.5 to 4
Outputs:
- residual: float32 [3072, 3072], P('row', 'col')
All inputs are finite; a program needn't handle non-finite values.
Results may differ from a plain program's by a relative error of at most 0.0021.
Values may be sent and summed in bfloat16 or wider, within the bound.
No kernel may reach another device: no remote copies, remote signals or barrier semaphores. Data moves between devices by JAX's collectives and lax.ppermute only.
A program may use at most 128 MiB of HBM per device.

v0:
```python
import jax
import jax.numpy as jnp
from jax import lax
from jax.sharding import PartitionSpec as P


def body(integrals, amplitudes, energies):
    rows_tile = integrals.shape[0]
    cols_tile = amplitudes.shape[1]
    n_row = lax.axis_size("row")
    n_col = lax.axis_size("col")
    block = rows_tile // n_col
    panel = lax.all_gather(integrals, "col", axis=1, tiled=True)
    ladder = jnp.dot(
        panel,
        lax.all_gather(amplitudes, "row", axis=0, tiled=True),
        preferred_element_type=jnp.float32,
    )
    rounded = ladder.astype(jnp.bfloat16)
    by_rows = lax.all_to_all(rounded, "col", split_axis=0, concat_axis=1, tiled=True)
    lifted = lax.all_to_all(by_rows, "row", split_axis=1, concat_axis=0, tiled=True)
    shaped = lifted.reshape(n_row, 1, block, n_col * block)
    settled = lax.all_to_all(shaped, "col", split_axis=0, concat_axis=1, tiled=True)
    partner = settled.reshape(n_row * block, n_col * block).T.astype(jnp.float32)
    row_start = lax.axis_index("row") * rows_tile
    col_start = lax.axis_index("col") * cols_tile
    row_energy = lax.dynamic_slice_in_dim(energies, row_start, rows_tile, 0)
    col_energy = lax.dynamic_slice_in_dim(energies, col_start, cols_tile, 0)
    return (ladder + partner) / (row_energy[:, None] + col_energy[None, :])


def solution(mesh):
    placed = (P("row", "col"), P("row", "col"), P())
    return jax.shard_map(
        body, mesh=mesh, in_specs=placed, out_specs=P("row", "col"), check_vma=False
    )
```

profile of v0, /device:TPU:0, one launch (start us, length us, event | category | flops | bytes accessed | tf_op | source)
XLA Modules:
  0.0 82.2 jit_solution(17657552466016372844)
XLA Ops:
  0.0 15.4 %all_gather.6 = bf16[384,192]{0,1:T(8,128)(2,1)S(1)} all-gather(bf16[384,48]{0,1:T(8,128)(2,1)} %param.3), channel_id=1, replica_groups=mesh['row'=8,'col'=4] {'col'}, dimensions={1}, use_global_device_ids=true | all-gather | bytes 184320 | tf_op jit(solution)/shard_map/all_gather | solution.py:13
  15.4 9.7 %all_gather.7 = bf16[192,768]{1,0:T(8,128)(2,1)S(1)} all-gather(bf16[24,768]{1,0:T(8,128)(2,1)} %param.4), channel_id=1, replica_groups=mesh['row'=8,'col'=4] {'row'}, dimensions={0}, use_global_device_ids=true | all-gather | bytes 331776 | tf_op jit(solution)/shard_map/all_gather | solution.py:16
  25.0 0.4 fusion.1
  25.4 21.2 %all_to_all.41 = bf16[4,96,768]{2,1,0:T(8,128)(2,1)S(1)} all-to-all(bf16[4,96,768]{2,1,0:T(8,128)(2,1)S(1)} %bitcast.23), channel_id=1, replica_groups=mesh['row'=8,'col'=4] {'col'}, dimensions={0} | all-to-all | bytes 1179648 | tf_op jit(solution)/shard_map/all_to_all | solution.py:20
  46.6 0.5 copy.8
  47.0 0.2 all_to_all.34
  47.2 0.1 copy.9
  47.3 0.0 copy-start
  47.3 13.5 %all_to_all.42 = bf16[96,8,384]{2,0,1:T(8,128)(2,1)} all-to-all(bf16[96,8,384]{2,0,1:T(8,128)(2,1)S(1)} %copy.9), channel_id=1, replica_groups=mesh['row'=8,'col'=4] {'row'}, dimensions={1} | all-to-all | bytes 1179648 | tf_op jit(solution)/shard_map/all_to_all | solution.py:21
  60.8 3.5 %all-to-all-start.2 = ((bf16[8,1,96,384]{3,2,1,0:T(8,128)(2,1)}), bf16[8,1,96,384]{3,2,1,0:T(8,128)(2,1)S(1)}, u32[]{:S(2)}, u32[]{:S(2)}) async-start(bf16[8,1,96,384]{3,2,1,0:T(8,128)(2,1)} %bitcast.4), calls=%async_computation.2 | async-start | bytes 1179648 | tf_op jit(solution)/shard_map/all_to_all | solution.py:23
  64.3 0.0 copy-done
  64.3 0.1 dynamic_slice.7
  64.4 0.1 dynamic_slice.6
  64.5 15.9 %all-to-all-done.2 = bf16[8,1,96,384]{3,2,1,0:T(8,128)(2,1)S(1)} async-done(((bf16[8,1,96,384]{3,2,1,0:T(8,128)(2,1)}), bf16[8,1,96,384]{3,2,1,0:T(8,128)(2,1)S(1)}, u32[]{:S(2)}, u32[]{:S(2)}) %all-to-all-start.2) | async-done | bytes 589856 | tf_op jit(solution)/shard_map/all_to_all | solution.py:23
  80.4 0.1 convert_bitcast_fusion
  80.5 0.1 copy.12
  80.5 0.4 copy.13
  80.9 1.2 %fusion = f32[384,768]{1,0:T(8,128)} fusion(f32[384,768]{1,0:T(8,128)S(1)} %get-tuple-element.6, f32[768,384]{0,1:T(8,128)S(1)} %copy.13, f32[768]{0:T(1024)S(1)} %dynamic_slice.7, f32[384]{0:T(512)S(1)} %dynamic_slice.6), kind=kLoop, calls=%fused_computation.2 | loop fusion | flops 884736 | bytes 3543552 | tf_op jit(solution)/shard_map/div | solution.py:29
Async XLA Ops:
  47.3 17.0 %copy-start = (f32[3072]{0:T(1024)S(1)}, f32[3072]{0:T(1024)}, u32[]{:S(2)}) copy-start(f32[3072]{0:T(1024)} %param.5) | copy-start | bytes 36868
  60.8 19.6 %all-to-all-start.2 = ((bf16[8,1,96,384]{3,2,1,0:T(8,128)(2,1)}), bf16[8,1,96,384]{3,2,1,0:T(8,128)(2,1)S(1)}, u32[]{:S(2)}, u32[]{:S(2)}) async-start(bf16[8,1,96,384]{3,2,1,0:T(8,128)(2,1)} %bitcast.4), calls=%async_computation.2 | async-start | bytes 1179648 | tf_op jit(solution)/shard_map/all_to_all | solution.py:23
where the time goes:
time: 82.5 us; the launch traced here: 82.2 us
  blocking collectives  59.7 us (72%)
  waiting for transfers between devices  15.9 us (19%)
  starting transfers between devices  3.48 us (4%)
  other arithmetic  1.32 us (2%)
  local copies, waits for them, and re-layouts  1.3 us (2%)
    all_to_all x1, blocking collectives, body(): lax.all_to_all(rounded, 'col', split_axis=0, concat_axis=1, tiled=True)  21.2 us
    all_to_all x1, waiting for transfers between devices, body(): lax.all_to_all(shaped, 'col', split_axis=0, concat_axis=1, tiled=True)  15.9 us
    all_gather x1, blocking collectives, body(): panel = lax.all_gather(integrals, 'col', axis=1, tiled=True)  15.4 us
    all_to_all x1, blocking collectives, body(): lax.all_to_all(by_rows, 'row', split_axis=1, concat_axis=0, tiled=True)  13.5 us
    all_gather x1, blocking collectives, body(): lax.all_gather(amplitudes, 'row', axis=0, tiled=True)  9.65 us
    all_to_all x1, starting transfers between devices, body(): lax.all_to_all(shaped, 'col', split_axis=0, concat_axis=1, tiled=True)  3.48 us
  transfers between devices with their start and end apart: 1, of which 1 were waited for; matrix products, arithmetic and copies ran while one was open for 0% of the time, Pallas kernels for 0%

commit v1 on v0

--- a/solution.py
+++ b/solution.py
@@ -1,10 +1,143 @@
+import functools
+
 import jax
 import jax.numpy as jnp
 from jax import lax
+from jax.experimental import pallas as pl
+from jax.experimental.pallas import tpu as pltpu
 from jax.sharding import PartitionSpec as P
 
+AXES = ("row", "col")
+TILE = 128
 
-def body(integrals, amplitudes, energies):
+
+def pick(index, pieces):
+    return functools.reduce(
+        lambda kept, i: jnp.where(index == i, pieces[i], kept),
+        range(1, len(pieces)),
+        pieces[0],
+    )
+
+
+def finish(n, kp, rt, *refs):
+    gathered, settled = refs[:n], refs[n : 2 * n]
+    swap_a, swap_b, energy, out, lhs, rhs, mir_l, mir_r, buffer, done = refs[2 * n :]
+    row, col = lax.axis_index("row"), lax.axis_index("col")
+    chip, core = row // 2, row % 2
+    shift = chip ^ col
+
+    @pl.when(core == 0)
+    def _():
+        for j in range(n):
+            own = pl.ds(pl.multiple_of((shift ^ j) * kp, kp), kp)
+            here = pl.ds(j * kp, kp)
+            base = 2 * kp * j
+            lhs[own, :] = gathered[j][:kp, :]
+            rhs[here, :rt] = swap_a[base : base + kp, :]
+            rhs[here, rt:] = swap_a[base + kp : base + 2 * kp, :]
+            mir_l[here, :] = settled[j][:kp, :]
+            mir_r[own, :rt] = swap_b[base : base + kp, :]
+            mir_r[own, rt:] = swap_b[base + kp : base + 2 * kp, :]
+
+    @pl.when(core == 1)
+    def _():
+        for j in range(n):
+            own = pl.ds(pl.multiple_of((shift ^ j) * kp, kp), kp)
+            here = pl.ds(j * kp, kp)
+            base = 2 * kp * j
+            lhs[own, :] = swap_a[base + kp : base + 2 * kp, :]
+            rhs[here, :rt] = gathered[j][2 * kp : 3 * kp, :]
+            rhs[here, rt:] = gathered[j][3 * kp :, :]
+            mir_l[here, :] = swap_b[base + kp : base + 2 * kp, :]
+            mir_r[own, :rt] = settled[j][:kp, :]
+            mir_r[own, rt:] = settled[j][kp:, :]
+
+    over_first = (((0,), (0,)), ((), ()))
+    across = energy[:, pl.ds(pl.multiple_of(col * 2 * rt, 2 * rt), 2 * rt)]
+    copies = []
+    for i in range(rt // TILE):
+        rows = slice(i * TILE, (i + 1) * TILE)
+        ladder = lax.dot_general(
+            lhs[:, rows], rhs[...], over_first, preferred_element_type=jnp.float32
+        )
+        partner = lax.dot_general(
+            mir_l[:, rows], mir_r[...], over_first, preferred_element_type=jnp.float32
+        )
+        partner = partner.astype(jnp.bfloat16).astype(jnp.float32)
+        along = energy[:, pl.ds(pl.multiple_of(row * rt + i * TILE, TILE), TILE)]
+        down = jnp.broadcast_to(along, (TILE, TILE)).T[:, :1]
+        buffer[rows, :] = (ladder + partner) / (down + across)
+        copies.append(pltpu.make_async_copy(buffer.at[rows], out.at[rows], done.at[i]))
+        copies[-1].start()
+    for copy in copies:
+        copy.wait()
+
+
+def paired(integrals, amplitudes, energies):
+    n = lax.axis_size("col")
+    rt, kp = integrals.shape
+    ka = amplitudes.shape[0]
+    row, col = lax.axis_index("row"), lax.axis_index("col")
+    chip, core = row // 2, row % 2
+    shift = chip ^ col
+    first = core == 0
+
+    def send(value, target):
+        pairs = [
+            ((2 * k + h) * n + c, (2 * tk + th) * n + tc)
+            for k in range(n)
+            for h in range(2)
+            for c in range(n)
+            for tk, th, tc in [target(k, h, c)]
+        ]
+        return lax.ppermute(value, AXES, pairs)
+
+    def other(k, h, c):
+        return k, 1 - h, c
+
+    own = jnp.concatenate([integrals.T, amplitudes[:, :rt], amplitudes[:, rt:]])
+    own = lax.optimization_barrier(own)
+    theirs = send(own, other)
+    block = jnp.concatenate(
+        [
+            jnp.where(first, x[low:high], y[low:high])
+            for low, high in ((0, kp), (kp, kp + ka), (kp + ka, kp + 2 * ka))
+            for x, y in ((own, theirs), (theirs, own))
+        ]
+    )
+    order = sorted(range(1, n), key=lambda j: bin(j).count("1"))
+    gathered = {0: block}
+    for j in order:
+        gathered[j] = send(block, lambda k, h, c: (k ^ j * h, h, c ^ j * (1 - h)))
+    gathered = [gathered[j] for j in range(n)]
+    onward = [jnp.where(first, g[2 * kp :], g[: 2 * kp]) for g in gathered]
+    settled = {0: pick(shift, onward)}
+    for j in order:
+        settled[j] = send(
+            pick(shift ^ j, onward), lambda k, h, c: (k ^ j * (1 - h), h, c ^ j * h)
+        )
+    settled = [settled[j] for j in range(n)]
+    swap_a = send(
+        jnp.concatenate([jnp.where(first, g[: 2 * kp], g[2 * kp :]) for g in gathered]), other
+    )
+    swap_b = send(jnp.concatenate(settled), other)
+    keep = pl.BlockSpec(memory_space=pltpu.VMEM)
+    inputs = [*gathered, *settled, swap_a, swap_b, energies.reshape(1, -1)]
+    return pl.pallas_call(
+        functools.partial(finish, n, kp, rt),
+        in_specs=[keep] * len(inputs),
+        out_specs=pl.BlockSpec(memory_space=pl.ANY),
+        out_shape=jax.ShapeDtypeStruct((rt, 2 * rt), jnp.float32),
+        scratch_shapes=[
+            *[pltpu.VMEM((n * kp, width), jnp.bfloat16) for width in (rt, 2 * rt, rt, 2 * rt)],
+            pltpu.VMEM((rt, 2 * rt), jnp.float32),
+            pltpu.SemaphoreType.DMA((rt // TILE,)),
+        ],
+        name="finish",
+    )(*[pltpu.with_memory_space_constraint(x, pltpu.VMEM) for x in inputs])
+
+
+def general(integrals, amplitudes, energies):
     rows_tile = integrals.shape[0]
     cols_tile = amplitudes.shape[1]
     n_row = lax.axis_size("row")
@@ -29,6 +162,19 @@
     return (ladder + partner) / (row_energy[:, None] + col_energy[None, :])
 
 
+def body(integrals, amplitudes, energies):
+    rt, kp = integrals.shape
+    n_row, n_col = lax.axis_size("row"), lax.axis_size("col")
+    fits = (
+        n_row == 2 * n_col
+        and n_col & (n_col - 1) == 0
+        and amplitudes.shape == (kp // 2, 2 * rt)
+        and rt % 128 == 0
+        and kp % 16 == 0
+    )
+    return (paired if fits else general)(integrals, amplitudes, energies)
+
+
 def solution(mesh):
     placed = (P("row", "col"), P("row", "col"), P())
     return jax.shard_map(

time: 82.5 us -> 28.4 us (0.34)
  blocking collectives: 59.7 us -> 0 us
  starting transfers between devices: 3.48 us -> 11.8 us
  waiting for transfers between devices: 15.9 us -> 12.9 us
  Pallas kernels: 0 us -> 1.45 us
    all_to_all x2 -> x0, blocking collectives: 34.7 us -> none  [the longest x1 21.2 us: body(): lax.all_to_all(rounded, 'col', split_axis=0, concat_axis=1, tiled=True)]
    all_gather x2 -> x0, blocking collectives: 25 us -> none  [the longest x1 15.4 us: body(): panel = lax.all_gather(integrals, 'col', axis=1, tiled=True)]
    all_to_all x1 -> x0, waiting for transfers between devices: 15.9 us -> none  [body(): lax.all_to_all(shaped, 'col', split_axis=0, concat_axis=1, tiled=True)]
    ppermute x0 -> x9, waiting for transfers between devices: none -> 12.9 us  [send(): return lax.ppermute(value, AXES, pairs)]
    ppermute x0 -> x9, starting transfers between devices: none -> 11.8 us  [send(): return lax.ppermute(value, AXES, pairs)]
    all_to_all x1 -> x0, starting transfers between devices: 3.48 us -> none  [body(): lax.all_to_all(shaped, 'col', split_axis=0, concat_axis=1, tiled=True)]
    pallas_call x0 -> x1, Pallas kernels: none -> 1.45 us  [paired(): pl.pallas_call(functools.partial(finish, n, kp, rt), in_specs=[keep] * le...]
    div x1 -> x0, other arithmetic: 1.24 us -> none  [body(): return (ladder + partner) / (row_energy[:, None] + col_energy[None, :])]
  transfers between devices with their start and end apart: 1 -> 9, of which waited for: 1 -> 7; matrix products, arithmetic and copies ran while one was open for 0% -> 1% of each run, Pallas kernels for 0% -> 0%
where the time goes in v1:
time: 28.4 us; the launch traced here: 28.2 us
  waiting for transfers between devices  12.9 us (45%)
  starting transfers between devices  11.8 us (42%)
  Pallas kernels  1.45 us (5%)
  other arithmetic  1.14 us (4%)
  local copies, waits for them, and re-layouts  0.75 us (3%)
    ppermute x9, waiting for transfers between devices, send(): return lax.ppermute(value, AXES, pairs)  12.9 us
    ppermute x9, starting transfers between devices, send(): return lax.ppermute(value, AXES, pairs)  11.8 us
    pallas_call x1, Pallas kernels, paired(): pl.pallas_call(functools.partial(finish, n, kp, rt), in_specs=[keep] * le...  1.45 us
    concatenate x1, other arithmetic, paired(): own = jnp.concatenate([integrals.T, amplitudes[:, :rt], amplitudes[:, rt:]])  0.78 us
    slice x1, local copies, waits for them, and re-layouts, paired(): own = jnp.concatenate([integrals.T, amplitudes[:, :rt], amplitudes[:, rt:]])  0.74 us
  transfers between devices with their start and end apart: 9, of which 7 were waited for; matrix products, arithmetic and copies ran while one was open for 1% of the time, Pallas kernels for 0%

profile of v1, /device:TPU:0, one launch (start us, length us, event | category | flops | bytes accessed | tf_op | source)
XLA Modules:
  0.0 28.2 jit_solution(404105855073546269)
XLA Ops:
  0.0 0.7 %fusion = (bf16[24,384]{1,0:T(8,128)(2,1)S(1)}, bf16[24,384]{1,0:T(8,128)(2,1)S(1)}) fusion(bf16[24,768]{1,0:T(8,128)(2,1)} %param.4), kind=kLoop, calls=%fused_computation.29 | loop fusion | bytes 73728 | tf_op jit(solution)/shard_map/slice | solution.py:98
  0.7 0.8 %pad_maximum_fusion.2 = bf16[96,384]{1,0:T(8,128)(2,1)S(1)} fusion(bf16[24,384]{1,0:T(8,128)(2,1)S(1)} %get-tuple-element.27, bf16[24,384]{1,0:T(8,128)(2,1)S(1)} %get-tuple-element.26, bf16[48,384]{1,0:T(8,128)(2,1)} %bitcast.3), kind=kLoop, calls=%fused_computation.2 | loop fusion | flops 221184 | bytes 147456 | tf_op jit(solution)/shard_map/concatenate | solution.py:98
  1.5 0.5 %collective-permute-start = (bf16[96,384]{1,0:T(8,128)(2,1)S(1)}, bf16[96,384]{1,0:T(8,128)(2,1)S(1)}, u32[]{:S(2)}, u32[]{:S(2)}) collective-permute-start(bf16[96,384]{1,0:T(8,128)(2,1)S(1)} %pad_maximum_fusion.2), channel_id=1, source_target_pairs={{0,4},{1,5},{2,6},{3,7},{4,0},{5,1},{6,2},{7,3},{8,12},{9,13},{10,... | collective-permute-start | bytes 221192 | tf_op jit(solution)/shard_map/ppermute | solution.py:93
  2.0 0.9 %collective-permute-done = bf16[96,384]{1,0:T(8,128)(2,1)S(1)} collective-permute-done((bf16[96,384]{1,0:T(8,128)(2,1)S(1)}, bf16[96,384]{1,0:T(8,128)(2,1)S(1)}, u32[]{:S(2)}, u32[]{:S(2)}) %collective-permute-start) | collective-permute-done | bytes 73760 | tf_op jit(solution)/shard_map/ppermute | solution.py:93
  3.1 5.0 %collective-permute-start.3 = (bf16[192,384]{1,0:T(8,128)(2,1)S(1)}, bf16[192,384]{1,0:T(8,128)(2,1)S(1)}, u32[]{:S(2)}, u32[]{:S(2)}) collective-permute-start(bf16[192,384]{1,0:T(8,128)(2,1)S(1)} %get-tuple-element.10.refs_0_), channel_id=1, source_target_pairs={{0,3},{1,2},{2,1},{3,0},{4,28},{5,29},{6,30},{7,31},{8,11},{9,10},... | collective-permute-start | bytes 442376 | tf_op jit(solution)/shard_map/ppermute | solution.py:93
  8.1 0.0 collective-permute-start.2
  8.1 0.6 %collective-permute-start.1 = (bf16[192,384]{1,0:T(8,128)(2,1)S(1)}, bf16[192,384]{1,0:T(8,128)(2,1)S(1)}, u32[]{:S(2)}, u32[]{:S(2)}) collective-permute-start(bf16[192,384]{1,0:T(8,128)(2,1)S(1)} %get-tuple-element.10.refs_0_), channel_id=1, source_target_pairs={{0,1},{1,0},{2,3},{3,2},{4,12},{5,13},{6,14},{7,15},{8,9},{9,8},{1... | collective-permute-start | bytes 442376 | tf_op jit(solution)/shard_map/ppermute | solution.py:93
  8.7 2.6 %collective-permute-done.3.refs_3_ = bf16[192,384]{1,0:T(8,128)(2,1)S(1)} collective-permute-done((bf16[192,384]{1,0:T(8,128)(2,1)S(1)}, bf16[192,384]{1,0:T(8,128)(2,1)S(1)}, u32[]{:S(2)}, u32[]{:S(2)}) %collective-permute-start.3) | collective-permute-done | bytes 147488 | tf_op jit(solution)/shard_map/ppermute | solution.py:93
  11.3 4.2 %collective-permute-done.2.refs_2_ = bf16[192,384]{1,0:T(8,128)(2,1)S(1)} collective-permute-done((bf16[192,384]{1,0:T(8,128)(2,1)S(1)}, bf16[192,384]{1,0:T(8,128)(2,1)S(1)}, u32[]{:S(2)}, u32[]{:S(2)}) %collective-permute-start.2) | collective-permute-done | bytes 147488 | tf_op jit(solution)/shard_map/ppermute | solution.py:93
  15.5 0.0 collective-permute-done.1.refs_1_
  15.5 0.1 select_select_fusion
  15.6 0.0 copy-start
  15.6 4.9 %collective-permute-start.6 = (bf16[96,384]{1,0:T(8,128)(2,1)S(1)}, bf16[96,384]{1,0:T(8,128)(2,1)S(1)}, u32[]{:S(2)}, u32[]{:S(2)}) collective-permute-start(bf16[96,384]{1,0:T(8,128)(2,1)S(1)} %get-tuple-element.5), channel_id=1, source_target_pairs={{0,24},{1,25},{2,26},{3,27},{4,7},{5,6},{6,5},{7,4},{8,16},{9,17},... | collective-permute-start | bytes 221192 | tf_op jit(solution)/shard_map/ppermute | solution.py:93
  20.5 0.1 collective-permute-start.5
  20.6 0.6 %collective-permute-start.4 = (bf16[96,384]{1,0:T(8,128)(2,1)S(1)}, bf16[96,384]{1,0:T(8,128)(2,1)S(1)}, u32[]{:S(2)}, u32[]{:S(2)}) collective-permute-start(bf16[96,384]{1,0:T(8,128)(2,1)S(1)} %get-tuple-element.23), channel_id=1, source_target_pairs={{0,8},{1,9},{2,10},{3,11},{4,5},{5,4},{6,7},{7,6},{8,0},{9,1},{10,... | collective-permute-start | bytes 221192 | tf_op jit(solution)/shard_map/ppermute | solution.py:93
  21.2 0.1 collective-permute-start.7
  21.3 1.5 %collective-permute-done.6.refs_7_ = bf16[96,384]{1,0:T(8,128)(2,1)S(1)} collective-permute-done((bf16[96,384]{1,0:T(8,128)(2,1)S(1)}, bf16[96,384]{1,0:T(8,128)(2,1)S(1)}, u32[]{:S(2)}, u32[]{:S(2)}) %collective-permute-start.6) | collective-permute-done | bytes 73760 | tf_op jit(solution)/shard_map/ppermute | solution.py:93
  22.8 2.1 %collective-permute-done.5.refs_6_ = bf16[96,384]{1,0:T(8,128)(2,1)S(1)} collective-permute-done((bf16[96,384]{1,0:T(8,128)(2,1)S(1)}, bf16[96,384]{1,0:T(8,128)(2,1)S(1)}, u32[]{:S(2)}, u32[]{:S(2)}) %collective-permute-start.5) | collective-permute-done | bytes 73760 | tf_op jit(solution)/shard_map/ppermute | solution.py:93
  24.9 0.1 collective-permute-done.4.refs_5_
  25.0 0.1 collective-permute-start.8
  25.1 0.0 collective-permute-done.7.refs_8_
  25.1 1.6 %collective-permute-done.8.refs_9_ = bf16[384,384]{1,0:T(8,128)(2,1)S(1)} collective-permute-done((bf16[384,384]{1,0:T(8,128)(2,1)S(1)}, bf16[384,384]{1,0:T(8,128)(2,1)S(1)}, u32[]{:S(2)}, u32[]{:S(2)}) %collective-permute-start.8) | collective-permute-done | bytes 294944 | tf_op jit(solution)/shard_map/ppermute | solution.py:93
  26.7 0.0 copy-done
  26.7 1.5 %finish.1 = f32[384,768]{1,0:T(8,128)} custom-call(bf16[192,384]{1,0:T(8,128)(2,1)S(1)} %get-tuple-element.10.refs_0_, bf16[192,384]{1,0:T(8,128)(2,1)S(1)} %collective-permute-done.1.refs_1_, bf16[192,384]{1,0:T(8,128)(2,1)S(1)} %collective-permute-done.2.refs_2_, bf16[192,384]{1,0:T(8,128)(2,1)S(1)} %collective-permute-done.3.refs_3_, ...), custom_call_target="tpu_custom_call" | custom-call | tf_op jit(solution)/shard_map/finish/pallas_call | solution.py:126
  (12 shorter events, 0.3 us)
Async XLA Ops:
  1.5 1.4 %collective-permute-start = (bf16[96,384]{1,0:T(8,128)(2,1)S(1)}, bf16[96,384]{1,0:T(8,128)(2,1)S(1)}, u32[]{:S(2)}, u32[]{:S(2)}) collective-permute-start(bf16[96,384]{1,0:T(8,128)(2,1)S(1)} %pad_maximum_fusion.2), channel_id=1, source_target_pairs={{0,4},{1,5},{2,6},{3,7},{4,0},{5,1},{6,2},{7,3},{8,12},{9,13},{10,... | collective-permute-start | bytes 221192 | tf_op jit(solution)/shard_map/ppermute | solution.py:93
  3.1 8.2 %collective-permute-start.3 = (bf16[192,384]{1,0:T(8,128)(2,1)S(1)}, bf16[192,384]{1,0:T(8,128)(2,1)S(1)}, u32[]{:S(2)}, u32[]{:S(2)}) collective-permute-start(bf16[192,384]{1,0:T(8,128)(2,1)S(1)} %get-tuple-element.10.refs_0_), channel_id=1, source_target_pairs={{0,3},{1,2},{2,1},{3,0},{4,28},{5,29},{6,30},{7,31},{8,11},{9,10},... | collective-permute-start | bytes 442376 | tf_op jit(solution)/shard_map/ppermute | solution.py:93
  8.1 7.4 %collective-permute-start.2 = (bf16[192,384]{1,0:T(8,128)(2,1)S(1)}, bf16[192,384]{1,0:T(8,128)(2,1)S(1)}, u32[]{:S(2)}, u32[]{:S(2)}) collective-permute-start(bf16[192,384]{1,0:T(8,128)(2,1)S(1)} %get-tuple-element.10.refs_0_), channel_id=1, source_target_pairs={{0,2},{1,3},{2,0},{3,1},{4,20},{5,21},{6,22},{7,23},{8,10},{9,11},... | collective-permute-start | bytes 442376 | tf_op jit(solution)/shard_map/ppermute | solution.py:93
  8.1 7.4 %collective-permute-start.1 = (bf16[192,384]{1,0:T(8,128)(2,1)S(1)}, bf16[192,384]{1,0:T(8,128)(2,1)S(1)}, u32[]{:S(2)}, u32[]{:S(2)}) collective-permute-start(bf16[192,384]{1,0:T(8,128)(2,1)S(1)} %get-tuple-element.10.refs_0_), channel_id=1, source_target_pairs={{0,1},{1,0},{2,3},{3,2},{4,12},{5,13},{6,14},{7,15},{8,9},{9,8},{1... | collective-permute-start | bytes 442376 | tf_op jit(solution)/shard_map/ppermute | solution.py:93
  15.6 11.1 %copy-start = (f32[3072]{0:T(1024)S(1)}, f32[3072]{0:T(1024)}, u32[]{:S(2)}) copy-start(f32[3072]{0:T(1024)} %param.5) | copy-start | bytes 36868
  15.6 7.2 %collective-permute-start.6 = (bf16[96,384]{1,0:T(8,128)(2,1)S(1)}, bf16[96,384]{1,0:T(8,128)(2,1)S(1)}, u32[]{:S(2)}, u32[]{:S(2)}) collective-permute-start(bf16[96,384]{1,0:T(8,128)(2,1)S(1)} %get-tuple-element.5), channel_id=1, source_target_pairs={{0,24},{1,25},{2,26},{3,27},{4,7},{5,6},{6,5},{7,4},{8,16},{9,17},... | collective-permute-start | bytes 221192 | tf_op jit(solution)/shard_map/ppermute | solution.py:93
  20.5 4.4 %collective-permute-start.5 = (bf16[96,384]{1,0:T(8,128)(2,1)S(1)}, bf16[96,384]{1,0:T(8,128)(2,1)S(1)}, u32[]{:S(2)}, u32[]{:S(2)}) collective-permute-start(bf16[96,384]{1,0:T(8,128)(2,1)S(1)} %get-tuple-element.22), channel_id=1, source_target_pairs={{0,16},{1,17},{2,18},{3,19},{4,6},{5,7},{6,4},{7,5},{8,24},{9,25},... | collective-permute-start | bytes 221192 | tf_op jit(solution)/shard_map/ppermute | solution.py:93
  20.6 4.4 %collective-permute-start.4 = (bf16[96,384]{1,0:T(8,128)(2,1)S(1)}, bf16[96,384]{1,0:T(8,128)(2,1)S(1)}, u32[]{:S(2)}, u32[]{:S(2)}) collective-permute-start(bf16[96,384]{1,0:T(8,128)(2,1)S(1)} %get-tuple-element.23), channel_id=1, source_target_pairs={{0,8},{1,9},{2,10},{3,11},{4,5},{5,4},{6,7},{7,6},{8,0},{9,1},{10,... | collective-permute-start | bytes 221192 | tf_op jit(solution)/shard_map/ppermute | solution.py:93
  21.2 3.9 %collective-permute-start.7 = (bf16[384,384]{1,0:T(8,128)(2,1)S(1)}, bf16[384,384]{1,0:T(8,128)(2,1)S(1)}, u32[]{:S(2)}, u32[]{:S(2)}) collective-permute-start(bf16[384,384]{1,0:T(8,128)(2,1)S(1)} %pad_maximum_fusion), channel_id=1, source_target_pairs={{0,4},{1,5},{2,6},{3,7},{4,0},{5,1},{6,2},{7,3},{8,12},{9,13},{10,... | collective-permute-start | bytes 884744 | tf_op jit(solution)/shard_map/ppermute | solution.py:93
  25.0 1.6 %collective-permute-start.8 = (bf16[384,384]{1,0:T(8,128)(2,1)S(1)}, bf16[384,384]{1,0:T(8,128)(2,1)S(1)}, u32[]{:S(2)}, u32[]{:S(2)}) collective-permute-start(bf16[384,384]{1,0:T(8,128)(2,1)S(1)} %pad_maximum_fusion.1), channel_id=1, source_target_pairs={{0,4},{1,5},{2,6},{3,7},{4,0},{5,1},{6,2},{7,3},{8,12},{9,13},{10,... | collective-permute-start | bytes 884744 | tf_op jit(solution)/shard_map/ppermute | solution.py:93

commit v2 on v1

--- a/solution.py
+++ b/solution.py
@@ -20,37 +20,46 @@
 
 
 def finish(n, kp, rt, *refs):
-    gathered, settled = refs[:n], refs[n : 2 * n]
-    swap_a, swap_b, energy, out, lhs, rhs, mir_l, mir_r, buffer, done = refs[2 * n :]
+    direct, settled = refs[: n - 1], refs[n - 1 : 2 * n - 2]
+    swap_d, swap_s, own_i, own_a, near_i, near_a, energy, out = refs[2 * n - 2 : 2 * n + 6]
+    lhs, rhs, mir_l, mir_r, buffer, done = refs[2 * n + 6 :]
     row, col = lax.axis_index("row"), lax.axis_index("col")
     chip, core = row // 2, row % 2
     shift = chip ^ col
 
-    @pl.when(core == 0)
-    def _():
-        for j in range(n):
-            own = pl.ds(pl.multiple_of((shift ^ j) * kp, kp), kp)
-            here = pl.ds(j * kp, kp)
-            base = 2 * kp * j
-            lhs[own, :] = gathered[j][:kp, :]
-            rhs[here, :rt] = swap_a[base : base + kp, :]
-            rhs[here, rt:] = swap_a[base + kp : base + 2 * kp, :]
-            mir_l[here, :] = settled[j][:kp, :]
-            mir_r[own, :rt] = swap_b[base : base + kp, :]
-            mir_r[own, rt:] = swap_b[base + kp : base + 2 * kp, :]
-
-    @pl.when(core == 1)
-    def _():
-        for j in range(n):
-            own = pl.ds(pl.multiple_of((shift ^ j) * kp, kp), kp)
-            here = pl.ds(j * kp, kp)
-            base = 2 * kp * j
-            lhs[own, :] = swap_a[base + kp : base + 2 * kp, :]
-            rhs[here, :rt] = gathered[j][2 * kp : 3 * kp, :]
-            rhs[here, rt:] = gathered[j][3 * kp :, :]
-            mir_l[here, :] = swap_b[base + kp : base + 2 * kp, :]
-            mir_r[own, :rt] = settled[j][:kp, :]
-            mir_r[own, rt:] = settled[j][kp:, :]
+    def put(j, i_half, a_lo, a_hi, a_half, i_lo, i_hi):
+        here = pl.ds(j * kp, kp)
+        moved = pl.ds(pl.multiple_of((shift ^ j) * kp, kp), kp)
+        lhs[moved, :] = i_half
+        rhs[here, :rt] = a_lo
+        rhs[here, rt:] = a_hi
+        mir_l[here, :] = a_half
+        mir_r[moved, :rt] = i_lo
+        mir_r[moved, rt:] = i_hi
+
+    for h in range(2):
+
+        @pl.when(core == h)
+        def _():
+            def part(ref, i):
+                return ref[i * kp : (i + 1) * kp, :]
+
+            put(
+                0,
+                part(own_i, h),
+                part(own_a, 0),
+                part(own_a, 1),
+                part(near_a, h),
+                part(near_i, 0),
+                part(near_i, 1),
+            )
+            for j in range(1, n):
+                mine = [part(x[j - 1], i) for x in (direct, settled) for i in range(2)]
+                gift = [part(x, 2 * (j - 1) + i) for x in (swap_d, swap_s) for i in range(2)]
+                if h == 0:
+                    put(j, gift[0], mine[0], mine[1], mine[2], gift[2], gift[3])
+                else:
+                    put(j, mine[1], gift[0], gift[1], gift[3], mine[2], mine[3])
 
     over_first = (((0,), (0,)), ((), ()))
     across = energy[:, pl.ds(pl.multiple_of(col * 2 * rt, 2 * rt), 2 * rt)]
@@ -95,34 +104,53 @@
     def other(k, h, c):
         return k, 1 - h, c
 
-    own = jnp.concatenate([integrals.T, amplitudes[:, :rt], amplitudes[:, rt:]])
-    own = lax.optimization_barrier(own)
-    theirs = send(own, other)
-    block = jnp.concatenate(
-        [
-            jnp.where(first, x[low:high], y[low:high])
-            for low, high in ((0, kp), (kp, kp + ka), (kp + ka, kp + 2 * ka))
-            for x, y in ((own, theirs), (theirs, own))
-        ]
-    )
-    order = sorted(range(1, n), key=lambda j: bin(j).count("1"))
-    gathered = {0: block}
+    def carrier(j):
+        return 1 - j % 2
+
+    their_i, their_a = send(integrals.T, other), send(amplitudes, other)
+    mine = lax.optimization_barrier(
+        jnp.concatenate([integrals.T, amplitudes[:, :rt], amplitudes[:, rt:]])
+    )
+    pairs = [
+        (mine[:kp], their_i),
+        (mine[kp : kp + ka], their_a[:, :rt]),
+        (mine[kp + ka :], their_a[:, rt:]),
+    ]
+    packs = [(jnp.where(first, x, y), jnp.where(first, y, x)) for x, y in pairs]
+    own_i = jnp.concatenate(packs[0])
+    own_a = jnp.concatenate(packs[1] + packs[2])
+    own = {h: jnp.where(core == h, own_a, own_i) for h in range(2)}
+    order = range(n - 1, 0, -1)
+    gathered, direct, settled = {0: own[carrier(0)]}, {}, {}
     for j in order:
-        gathered[j] = send(block, lambda k, h, c: (k ^ j * h, h, c ^ j * (1 - h)))
-    gathered = [gathered[j] for j in range(n)]
-    onward = [jnp.where(first, g[2 * kp :], g[: 2 * kp]) for g in gathered]
-    settled = {0: pick(shift, onward)}
+        gathered[j] = send(
+            own[carrier(j)],
+            lambda k, h, c: (k, h, c ^ j) if h == carrier(j) else (k ^ j, h, c),
+        )
+    for j in order:
+        direct[j] = send(
+            own[carrier(j)],
+            lambda k, h, c: (k ^ j, 0, c) if h == carrier(j) else (k, 1, c ^ j),
+        )
     for j in order:
         settled[j] = send(
-            pick(shift ^ j, onward), lambda k, h, c: (k ^ j * (1 - h), h, c ^ j * h)
-        )
-    settled = [settled[j] for j in range(n)]
-    swap_a = send(
-        jnp.concatenate([jnp.where(first, g[: 2 * kp], g[2 * kp :]) for g in gathered]), other
-    )
-    swap_b = send(jnp.concatenate(settled), other)
+            pick(shift ^ j, gathered),
+            lambda k, h, c: (k ^ j, 0, c) if h == carrier(k ^ c ^ j) else (k, 1, c ^ j),
+        )
+    near = pick(shift, gathered)
+    far = send(near, other)
+    has_a = functools.reduce(
+        lambda kept, m: jnp.where(shift == m, core == carrier(m), kept), range(n), first
+    )
+    near_a, near_i = jnp.where(has_a, near, far), jnp.where(has_a, far, near)
+    direct, settled = [[x[j] for j in range(1, n)] for x in (direct, settled)]
+    swap_d, swap_s = send(jnp.concatenate(direct), other), send(jnp.concatenate(settled), other)
     keep = pl.BlockSpec(memory_space=pltpu.VMEM)
-    inputs = [*gathered, *settled, swap_a, swap_b, energies.reshape(1, -1)]
+    inputs = [
+        *direct,
+        *settled,
+        *[swap_d, swap_s, own_i, own_a, near_i, near_a, energies.reshape(1, -1)],
+    ]
     return pl.pallas_call(
         functools.partial(finish, n, kp, rt),
         in_specs=[keep] * len(inputs),

time: 28.4 us -> 24.5 us (0.86)
  waiting for transfers between devices: 12.9 us -> 3.44 us
  starting transfers between devices: 11.8 us -> 17.5 us
    ppermute x9 -> x14, waiting for transfers between devices: 12.9 us -> 3.44 us  [send(): return lax.ppermute(value, AXES, pairs)]
    ppermute x9 -> x14, starting transfers between devices: 11.8 us -> 17.5 us  [send(): return lax.ppermute(value, AXES, pairs)]
  transfers between devices with their start and end apart: 9 -> 14, of which waited for: 7 -> 3; matrix products, arithmetic and copies ran while one was open for 1% -> 7% of each run, Pallas kernels for 0% -> 0%
where the time goes in v2:
time: 24.5 us; the launch traced here: 24.3 us
  starting transfers between devices  17.5 us (71%)
  waiting for transfers between devices  3.44 us (14%)
  Pallas kernels  1.45 us (6%)
  other arithmetic  0.98 us (4%)
  local copies, waits for them, and re-layouts  0.75 us (3%)
    ppermute x14, starting transfers between devices, send(): return lax.ppermute(value, AXES, pairs)  17.5 us
    ppermute x14, waiting for transfers between devices, send(): return lax.ppermute(value, AXES, pairs)  3.44 us
    pallas_call x1, Pallas kernels, paired(): pl.pallas_call(functools.partial(finish, n, kp, rt), in_specs=[keep] * le...  1.45 us
    concatenate x1, other arithmetic, paired(): jnp.concatenate([integrals.T, amplitudes[:, :rt], amplitudes[:, rt:]])  0.78 us
    slice x1, local copies, waits for them, and re-layouts, paired(): amplitudes[:, :rt]  0.74 us
  transfers between devices with their start and end apart: 14, of which 3 were waited for; matrix products, arithmetic and copies ran while one was open for 7% of the time, Pallas kernels for 0%

profile of v2, /device:TPU:0, one launch (start us, length us, event | category | flops | bytes accessed | tf_op | source)
XLA Modules:
  0.0 24.3 jit_solution(12263105340115697447)
XLA Ops:
  0.0 0.5 %collective-permute-start.1 = (bf16[48,384]{1,0:T(8,128)(2,1)}, bf16[48,384]{1,0:T(8,128)(2,1)S(1)}, u32[]{:S(2)}, u32[]{:S(2)}) collective-permute-start(bf16[48,384]{1,0:T(8,128)(2,1)} %bitcast.3), channel_id=1, source_target_pairs={{0,4},{1,5},{2,6},{3,7},{4,0},{5,1},{6,2},{7,3},{8,12},{9,13},{10,... | collective-permute-start | bytes 110600 | tf_op jit(solution)/shard_map/ppermute | solution.py:102
  0.5 0.0 collective-permute-start
  0.5 0.7 %fusion = (bf16[24,384]{1,0:T(8,128)(2,1)S(1)}, bf16[24,384]{1,0:T(8,128)(2,1)S(1)}) fusion(bf16[24,768]{1,0:T(8,128)(2,1)} %param.4), kind=kLoop, calls=%fused_computation.19 | loop fusion | bytes 73728 | tf_op jit(solution)/shard_map/slice | solution.py:112
  1.3 0.8 %pad_maximum_fusion.2 = bf16[96,384]{1,0:T(8,128)(2,1)S(1)} fusion(bf16[24,384]{1,0:T(8,128)(2,1)S(1)} %get-tuple-element.21, bf16[24,384]{1,0:T(8,128)(2,1)S(1)} %get-tuple-element.20, bf16[48,384]{1,0:T(8,128)(2,1)} %bitcast.4), kind=kLoop, calls=%fused_computation.2 | loop fusion | flops 221184 | bytes 147456 | tf_op jit(solution)/shard_map/concatenate | solution.py:112
  2.1 0.0 collective-permute-done
  2.1 0.0 copy-start
  2.1 3.1 %collective-permute-start.6 = (bf16[96,384]{1,0:T(8,128)(2,1)S(1)}, bf16[96,384]{1,0:T(8,128)(2,1)S(1)}, u32[]{:S(2)}, u32[]{:S(2)}) collective-permute-start(bf16[96,384]{1,0:T(8,128)(2,1)S(1)} %get-tuple-element.11), channel_id=1, source_target_pairs={{0,16},{1,17},{2,18},{3,19},{4,6},{5,7},{6,4},{7,5},{8,24},{9,25},... | collective-permute-start | bytes 221192 | tf_op jit(solution)/shard_map/ppermute | solution.py:102
  5.2 0.7 %collective-permute-start.3 = (bf16[96,384]{1,0:T(8,128)(2,1)S(1)}, bf16[96,384]{1,0:T(8,128)(2,1)S(1)}, u32[]{:S(2)}, u32[]{:S(2)}) collective-permute-start(bf16[96,384]{1,0:T(8,128)(2,1)S(1)} %get-tuple-element.11), channel_id=1, source_target_pairs={{0,6},{1,7},{2,4},{3,5},{4,16},{5,17},{6,18},{7,19},{8,14},{9,15},... | collective-permute-start | bytes 221192 | tf_op jit(solution)/shard_map/ppermute | solution.py:102
  5.9 1.6 %collective-permute-start.7 = (bf16[96,384]{1,0:T(8,128)(2,1)S(1)}, bf16[96,384]{1,0:T(8,128)(2,1)S(1)}, u32[]{:S(2)}, u32[]{:S(2)}) collective-permute-start(bf16[96,384]{1,0:T(8,128)(2,1)S(1)} %get-tuple-element.12), channel_id=1, source_target_pairs={{0,1},{1,0},{2,3},{3,2},{4,12},{5,13},{6,14},{7,15},{8,9},{9,8},{1... | collective-permute-start | bytes 221192 | tf_op jit(solution)/shard_map/ppermute | solution.py:102
  7.5 2.5 %collective-permute-start.5 = (bf16[96,384]{1,0:T(8,128)(2,1)S(1)}, bf16[96,384]{1,0:T(8,128)(2,1)S(1)}, u32[]{:S(2)}, u32[]{:S(2)}) collective-permute-start(bf16[96,384]{1,0:T(8,128)(2,1)S(1)} %get-tuple-element.12), channel_id=1, source_target_pairs={{0,3},{1,2},{2,1},{3,0},{4,28},{5,29},{6,30},{7,31},{8,11},{9,10},... | collective-permute-start | bytes 221192 | tf_op jit(solution)/shard_map/ppermute | solution.py:102
  10.0 2.4 %collective-permute-start.4 = (bf16[96,384]{1,0:T(8,128)(2,1)S(1)}, bf16[96,384]{1,0:T(8,128)(2,1)S(1)}, u32[]{:S(2)}, u32[]{:S(2)}) collective-permute-start(bf16[96,384]{1,0:T(8,128)(2,1)S(1)} %get-tuple-element.12), channel_id=1, source_target_pairs={{0,24},{1,25},{2,26},{3,27},{4,7},{5,6},{6,5},{7,4},{8,16},{9,17},... | collective-permute-start | bytes 221192 | tf_op jit(solution)/shard_map/ppermute | solution.py:102
  12.5 0.0 collective-permute-done.6
  12.5 0.6 %collective-permute-start.2 = (bf16[96,384]{1,0:T(8,128)(2,1)S(1)}, bf16[96,384]{1,0:T(8,128)(2,1)S(1)}, u32[]{:S(2)}, u32[]{:S(2)}) collective-permute-start(bf16[96,384]{1,0:T(8,128)(2,1)S(1)} %get-tuple-element.12), channel_id=1, source_target_pairs={{0,8},{1,9},{2,10},{3,11},{4,5},{5,4},{6,7},{7,6},{8,0},{9,1},{10,... | collective-permute-start | bytes 221192 | tf_op jit(solution)/shard_map/ppermute | solution.py:102
  13.1 1.5 %collective-permute-done.5 = bf16[96,384]{1,0:T(8,128)(2,1)S(1)} collective-permute-done((bf16[96,384]{1,0:T(8,128)(2,1)S(1)}, bf16[96,384]{1,0:T(8,128)(2,1)S(1)}, u32[]{:S(2)}, u32[]{:S(2)}) %collective-permute-start.5) | collective-permute-done | bytes 73760 | tf_op jit(solution)/shard_map/ppermute | solution.py:102
  14.5 0.1 select_select_fusion
  14.6 2.3 %collective-permute-start.10 = (bf16[96,384]{1,0:T(8,128)(2,1)S(1)}, bf16[96,384]{1,0:T(8,128)(2,1)S(1)}, u32[]{:S(2)}, u32[]{:S(2)}) collective-permute-start(bf16[96,384]{1,0:T(8,128)(2,1)S(1)} %get-tuple-element.6), channel_id=1, source_target_pairs={{0,24},{1,6},{2,26},{3,4},{4,7},{5,25},{6,5},{7,27},{8,15},{9,17},... | collective-permute-start | bytes 221192 | tf_op jit(solution)/shard_map/ppermute | solution.py:102
  16.9 0.6 %collective-permute-start.8 = (bf16[96,384]{1,0:T(8,128)(2,1)S(1)}, bf16[96,384]{1,0:T(8,128)(2,1)S(1)}, u32[]{:S(2)}, u32[]{:S(2)}) collective-permute-start(bf16[96,384]{1,0:T(8,128)(2,1)S(1)} %get-tuple-element.8), channel_id=1, source_target_pairs={{0,8},{1,4},{2,10},{3,6},{4,5},{5,9},{6,7},{7,11},{8,13},{9,1},{10... | collective-permute-start | bytes 221192 | tf_op jit(solution)/shard_map/ppermute | solution.py:102
  17.5 2.1 %collective-permute-start.13 = (bf16[96,384]{1,0:T(8,128)(2,1)S(1)}, bf16[96,384]{1,0:T(8,128)(2,1)S(1)}, u32[]{:S(2)}, u32[]{:S(2)}) collective-permute-start(bf16[96,384]{1,0:T(8,128)(2,1)S(1)} %get-tuple-element.5), channel_id=1, source_target_pairs={{0,4},{1,5},{2,6},{3,7},{4,0},{5,1},{6,2},{7,3},{8,12},{9,13},{10,... | collective-permute-start | bytes 221192 | tf_op jit(solution)/shard_map/ppermute | solution.py:102
  19.7 0.1 collective-permute-start.11
  19.8 0.9 %collective-permute-done.9.refs_4_ = bf16[96,384]{1,0:T(8,128)(2,1)S(1)} collective-permute-done((bf16[96,384]{1,0:T(8,128)(2,1)S(1)}, bf16[96,384]{1,0:T(8,128)(2,1)S(1)}, u32[]{:S(2)}, u32[]{:S(2)}) %collective-permute-start.9) | collective-permute-done | bytes 73760 | tf_op jit(solution)/shard_map/ppermute | solution.py:102
  20.7 0.0 collective-permute-done.8.refs_3_
  20.7 1.0 %collective-permute-start.12 = (bf16[288,384]{1,0:T(8,128)(2,1)S(1)}, bf16[288,384]{1,0:T(8,128)(2,1)S(1)}, u32[]{:S(2)}, u32[]{:S(2)}) collective-permute-start(bf16[288,384]{1,0:T(8,128)(2,1)S(1)} %pad_maximum_fusion.1), channel_id=1, source_target_pairs={{0,4},{1,5},{2,6},{3,7},{4,0},{5,1},{6,2},{7,3},{8,12},{9,13},{10,... | collective-permute-start | bytes 663560 | tf_op jit(solution)/shard_map/ppermute | solution.py:102
  21.7 1.1 %collective-permute-done.12.refs_7_ = bf16[288,384]{1,0:T(8,128)(2,1)S(1)} collective-permute-done((bf16[288,384]{1,0:T(8,128)(2,1)S(1)}, bf16[288,384]{1,0:T(8,128)(2,1)S(1)}, u32[]{:S(2)}, u32[]{:S(2)}) %collective-permute-start.12) | collective-permute-done | bytes 221216 | tf_op jit(solution)/shard_map/ppermute | solution.py:102
  22.8 1.5 %finish.1 = f32[384,768]{1,0:T(8,128)} custom-call(bf16[96,384]{1,0:T(8,128)(2,1)S(1)} %collective-permute-done.2.refs_0_, bf16[96,384]{1,0:T(8,128)(2,1)S(1)} %collective-permute-done.3.refs_1_, bf16[96,384]{1,0:T(8,128)(2,1)S(1)} %collective-permute-done.4.refs_2_, bf16[96,384]{1,0:T(8,128)(2,1)S(1)} %collective-permute-done.8.refs_3_, ...), custom_call_target="tpu_custom_call" | custom-call | tf_op jit(solution)/shard_map/finish/pallas_call | solution.py:154
  (17 shorter events, 0.2 us)
Async XLA Ops:
  0.0 2.0 %collective-permute-start.1 = (bf16[48,384]{1,0:T(8,128)(2,1)}, bf16[48,384]{1,0:T(8,128)(2,1)S(1)}, u32[]{:S(2)}, u32[]{:S(2)}) collective-permute-start(bf16[48,384]{1,0:T(8,128)(2,1)} %bitcast.3), channel_id=1, source_target_pairs={{0,4},{1,5},{2,6},{3,7},{4,0},{5,1},{6,2},{7,3},{8,12},{9,13},{10,... | collective-permute-start | bytes 110600 | tf_op jit(solution)/shard_map/ppermute | solution.py:102
  0.5 1.6 %collective-permute-start = (bf16[24,768]{1,0:T(8,128)(2,1)}, bf16[24,768]{1,0:T(8,128)(2,1)S(1)}, u32[]{:S(2)}, u32[]{:S(2)}) collective-permute-start(bf16[24,768]{1,0:T(8,128)(2,1)} %param.4), channel_id=1, source_target_pairs={{0,4},{1,5},{2,6},{3,7},{4,0},{5,1},{6,2},{7,3},{8,12},{9,13},{10,... | collective-permute-start | bytes 110600 | tf_op jit(solution)/shard_map/ppermute | solution.py:102
  2.1 20.7 %copy-start = (f32[3072]{0:T(1024)S(1)}, f32[3072]{0:T(1024)}, u32[]{:S(2)}) copy-start(f32[3072]{0:T(1024)} %param.5) | copy-start | bytes 36868
  2.1 10.3 %collective-permute-start.6 = (bf16[96,384]{1,0:T(8,128)(2,1)S(1)}, bf16[96,384]{1,0:T(8,128)(2,1)S(1)}, u32[]{:S(2)}, u32[]{:S(2)}) collective-permute-start(bf16[96,384]{1,0:T(8,128)(2,1)S(1)} %get-tuple-element.11), channel_id=1, source_target_pairs={{0,16},{1,17},{2,18},{3,19},{4,6},{5,7},{6,4},{7,5},{8,24},{9,25},... | collective-permute-start | bytes 221192 | tf_op jit(solution)/shard_map/ppermute | solution.py:102
  5.2 11.7 %collective-permute-start.3 = (bf16[96,384]{1,0:T(8,128)(2,1)S(1)}, bf16[96,384]{1,0:T(8,128)(2,1)S(1)}, u32[]{:S(2)}, u32[]{:S(2)}) collective-permute-start(bf16[96,384]{1,0:T(8,128)(2,1)S(1)} %get-tuple-element.11), channel_id=1, source_target_pairs={{0,6},{1,7},{2,4},{3,5},{4,16},{5,17},{6,18},{7,19},{8,14},{9,15},... | collective-permute-start | bytes 221192 | tf_op jit(solution)/shard_map/ppermute | solution.py:102
  5.9 7.1 %collective-permute-start.7 = (bf16[96,384]{1,0:T(8,128)(2,1)S(1)}, bf16[96,384]{1,0:T(8,128)(2,1)S(1)}, u32[]{:S(2)}, u32[]{:S(2)}) collective-permute-start(bf16[96,384]{1,0:T(8,128)(2,1)S(1)} %get-tuple-element.12), channel_id=1, source_target_pairs={{0,1},{1,0},{2,3},{3,2},{4,12},{5,13},{6,14},{7,15},{8,9},{9,8},{1... | collective-permute-start | bytes 221192 | tf_op jit(solution)/shard_map/ppermute | solution.py:102
  7.5 7.0 %collective-permute-start.5 = (bf16[96,384]{1,0:T(8,128)(2,1)S(1)}, bf16[96,384]{1,0:T(8,128)(2,1)S(1)}, u32[]{:S(2)}, u32[]{:S(2)}) collective-permute-start(bf16[96,384]{1,0:T(8,128)(2,1)S(1)} %get-tuple-element.12), channel_id=1, source_target_pairs={{0,3},{1,2},{2,1},{3,0},{4,28},{5,29},{6,30},{7,31},{8,11},{9,10},... | collective-permute-start | bytes 221192 | tf_op jit(solution)/shard_map/ppermute | solution.py:102
  10.0 7.6 %collective-permute-start.4 = (bf16[96,384]{1,0:T(8,128)(2,1)S(1)}, bf16[96,384]{1,0:T(8,128)(2,1)S(1)}, u32[]{:S(2)}, u32[]{:S(2)}) collective-permute-start(bf16[96,384]{1,0:T(8,128)(2,1)S(1)} %get-tuple-element.12), channel_id=1, source_target_pairs={{0,24},{1,25},{2,26},{3,27},{4,7},{5,6},{6,5},{7,4},{8,16},{9,17},... | collective-permute-start | bytes 221192 | tf_op jit(solution)/shard_map/ppermute | solution.py:102
  12.5 7.2 %collective-permute-start.2 = (bf16[96,384]{1,0:T(8,128)(2,1)S(1)}, bf16[96,384]{1,0:T(8,128)(2,1)S(1)}, u32[]{:S(2)}, u32[]{:S(2)}) collective-permute-start(bf16[96,384]{1,0:T(8,128)(2,1)S(1)} %get-tuple-element.12), channel_id=1, source_target_pairs={{0,8},{1,9},{2,10},{3,11},{4,5},{5,4},{6,7},{7,6},{8,0},{9,1},{10,... | collective-permute-start | bytes 221192 | tf_op jit(solution)/shard_map/ppermute | solution.py:102
  14.6 5.2 %collective-permute-start.10 = (bf16[96,384]{1,0:T(8,128)(2,1)S(1)}, bf16[96,384]{1,0:T(8,128)(2,1)S(1)}, u32[]{:S(2)}, u32[]{:S(2)}) collective-permute-start(bf16[96,384]{1,0:T(8,128)(2,1)S(1)} %get-tuple-element.6), channel_id=1, source_target_pairs={{0,24},{1,6},{2,26},{3,4},{4,7},{5,25},{6,5},{7,27},{8,15},{9,17},... | collective-permute-start | bytes 221192 | tf_op jit(solution)/shard_map/ppermute | solution.py:102
  16.9 3.8 %collective-permute-start.9 = (bf16[96,384]{1,0:T(8,128)(2,1)S(1)}, bf16[96,384]{1,0:T(8,128)(2,1)S(1)}, u32[]{:S(2)}, u32[]{:S(2)}) collective-permute-start(bf16[96,384]{1,0:T(8,128)(2,1)S(1)} %get-tuple-element.7), channel_id=1, source_target_pairs={{0,6},{1,17},{2,4},{3,19},{4,16},{5,7},{6,18},{7,5},{8,24},{9,15},... | collective-permute-start | bytes 221192 | tf_op jit(solution)/shard_map/ppermute | solution.py:102
  16.9 3.8 %collective-permute-start.8 = (bf16[96,384]{1,0:T(8,128)(2,1)S(1)}, bf16[96,384]{1,0:T(8,128)(2,1)S(1)}, u32[]{:S(2)}, u32[]{:S(2)}) collective-permute-start(bf16[96,384]{1,0:T(8,128)(2,1)S(1)} %get-tuple-element.8), channel_id=1, source_target_pairs={{0,8},{1,4},{2,10},{3,6},{4,5},{5,9},{6,7},{7,11},{8,13},{9,1},{10... | collective-permute-start | bytes 221192 | tf_op jit(solution)/shard_map/ppermute | solution.py:102
  17.5 4.1 %collective-permute-start.13 = (bf16[96,384]{1,0:T(8,128)(2,1)S(1)}, bf16[96,384]{1,0:T(8,128)(2,1)S(1)}, u32[]{:S(2)}, u32[]{:S(2)}) collective-permute-start(bf16[96,384]{1,0:T(8,128)(2,1)S(1)} %get-tuple-element.5), channel_id=1, source_target_pairs={{0,4},{1,5},{2,6},{3,7},{4,0},{5,1},{6,2},{7,3},{8,12},{9,13},{10,... | collective-permute-start | bytes 221192 | tf_op jit(solution)/shard_map/ppermute | solution.py:102
  19.7 2.0 %collective-permute-start.11 = (bf16[288,384]{1,0:T(8,128)(2,1)S(1)}, bf16[288,384]{1,0:T(8,128)(2,1)S(1)}, u32[]{:S(2)}, u32[]{:S(2)}) collective-permute-start(bf16[288,384]{1,0:T(8,128)(2,1)S(1)} %pad_maximum_fusion), channel_id=1, source_target_pairs={{0,4},{1,5},{2,6},{3,7},{4,0},{5,1},{6,2},{7,3},{8,12},{9,13},{10,... | collective-permute-start | bytes 663560 | tf_op jit(solution)/shard_map/ppermute | solution.py:102
  20.7 2.1 %collective-permute-start.12 = (bf16[288,384]{1,0:T(8,128)(2,1)S(1)}, bf16[288,384]{1,0:T(8,128)(2,1)S(1)}, u32[]{:S(2)}, u32[]{:S(2)}) collective-permute-start(bf16[288,384]{1,0:T(8,128)(2,1)S(1)} %pad_maximum_fusion.1), channel_id=1, source_target_pairs={{0,4},{1,5},{2,6},{3,7},{4,0},{5,1},{6,2},{7,3},{8,12},{9,13},{10,... | collective-permute-start | bytes 663560 | tf_op jit(solution)/shard_map/ppermute | solution.py:102

commit v3 on v2

--- a/solution.py
+++ b/solution.py
@@ -6,6 +6,7 @@
 from jax.experimental import pallas as pl
 from jax.experimental.pallas import tpu as pltpu
 from jax.sharding import PartitionSpec as P
+
 
 AXES = ("row", "col")
 TILE = 128
@@ -124,13 +125,11 @@
     gathered, direct, settled = {0: own[carrier(0)]}, {}, {}
     for j in order:
         gathered[j] = send(
-            own[carrier(j)],
-            lambda k, h, c: (k, h, c ^ j) if h == carrier(j) else (k ^ j, h, c),
+            own[carrier(j)], lambda k, h, c: (k, h, c ^ j) if h == carrier(j) else (k ^ j, h, c)
         )
     for j in order:
         direct[j] = send(
-            own[carrier(j)],
-            lambda k, h, c: (k ^ j, 0, c) if h == carrier(j) else (k, 1, c ^ j),
+            own[carrier(j)], lambda k, h, c: (k ^ j, 0, c) if h == carrier(j) else (k, 1, c ^ j)
         )
     for j in order:
         settled[j] = send(

time: 24.5 us -> 24.5 us (level)
  no operation moved by 1% of the time
where the time goes in v3:
time: 24.5 us; the launch traced here: 24.3 us
  starting transfers between devices  17.5 us (71%)
  waiting for transfers between devices  3.44 us (14%)
  Pallas kernels  1.45 us (6%)
  other arithmetic  0.98 us (4%)
  local copies, waits for them, and re-layouts  0.75 us (3%)
    ppermute x14, starting transfers between devices, send(): return lax.ppermute(value, AXES, pairs)  17.5 us
    ppermute x14, waiting for transfers between devices, send(): return lax.ppermute(value, AXES, pairs)  3.44 us
    pallas_call x1, Pallas kernels, paired(): pl.pallas_call(functools.partial(finish, n, kp, rt), in_specs=[keep] * le...  1.45 us
    concatenate x1, other arithmetic, paired(): jnp.concatenate([integrals.T, amplitudes[:, :rt], amplitudes[:, rt:]])  0.78 us
    slice x1, local copies, waits for them, and re-layouts, paired(): amplitudes[:, :rt]  0.74 us
  transfers between devices with their start and end apart: 14, of which 3 were waited for; matrix products, arithmetic and copies ran while one was open for 7% of the time, Pallas kernels for 0%

profile of v3, /device:TPU:0, one launch (start us, length us, event | category | flops | bytes accessed | tf_op | source)
XLA Modules:
  0.0 24.3 jit_solution(12263105340115697447)
XLA Ops:
  0.0 0.5 %collective-permute-start.1 = (bf16[48,384]{1,0:T(8,128)(2,1)}, bf16[48,384]{1,0:T(8,128)(2,1)S(1)}, u32[]{:S(2)}, u32[]{:S(2)}) collective-permute-start(bf16[48,384]{1,0:T(8,128)(2,1)} %bitcast.3), channel_id=1, source_target_pairs={{0,4},{1,5},{2,6},{3,7},{4,0},{5,1},{6,2},{7,3},{8,12},{9,13},{10,... | collective-permute-start | bytes 110600 | tf_op jit(solution)/shard_map/ppermute | solution.py:103
  0.5 0.0 collective-permute-start
  0.5 0.7 %fusion = (bf16[24,384]{1,0:T(8,128)(2,1)S(1)}, bf16[24,384]{1,0:T(8,128)(2,1)S(1)}) fusion(bf16[24,768]{1,0:T(8,128)(2,1)} %param.4), kind=kLoop, calls=%fused_computation.19 | loop fusion | bytes 73728 | tf_op jit(solution)/shard_map/slice | solution.py:113
  1.3 0.8 %pad_maximum_fusion.2 = bf16[96,384]{1,0:T(8,128)(2,1)S(1)} fusion(bf16[24,384]{1,0:T(8,128)(2,1)S(1)} %get-tuple-element.21, bf16[24,384]{1,0:T(8,128)(2,1)S(1)} %get-tuple-element.20, bf16[48,384]{1,0:T(8,128)(2,1)} %bitcast.4), kind=kLoop, calls=%fused_computation.2 | loop fusion | flops 221184 | bytes 147456 | tf_op jit(solution)/shard_map/concatenate | solution.py:113
  2.0 0.0 collective-permute-done.1
  2.1 0.0 collective-permute-done
  2.1 0.0 copy-start
  2.1 3.1 %collective-permute-start.6 = (bf16[96,384]{1,0:T(8,128)(2,1)S(1)}, bf16[96,384]{1,0:T(8,128)(2,1)S(1)}, u32[]{:S(2)}, u32[]{:S(2)}) collective-permute-start(bf16[96,384]{1,0:T(8,128)(2,1)S(1)} %get-tuple-element.11), channel_id=1, source_target_pairs={{0,16},{1,17},{2,18},{3,19},{4,6},{5,7},{6,4},{7,5},{8,24},{9,25},... | collective-permute-start | bytes 221192 | tf_op jit(solution)/shard_map/ppermute | solution.py:103
  5.2 0.7 %collective-permute-start.3 = (bf16[96,384]{1,0:T(8,128)(2,1)S(1)}, bf16[96,384]{1,0:T(8,128)(2,1)S(1)}, u32[]{:S(2)}, u32[]{:S(2)}) collective-permute-start(bf16[96,384]{1,0:T(8,128)(2,1)S(1)} %get-tuple-element.11), channel_id=1, source_target_pairs={{0,6},{1,7},{2,4},{3,5},{4,16},{5,17},{6,18},{7,19},{8,14},{9,15},... | collective-permute-start | bytes 221192 | tf_op jit(solution)/shard_map/ppermute | solution.py:103
  5.9 1.6 %collective-permute-start.7 = (bf16[96,384]{1,0:T(8,128)(2,1)S(1)}, bf16[96,384]{1,0:T(8,128)(2,1)S(1)}, u32[]{:S(2)}, u32[]{:S(2)}) collective-permute-start(bf16[96,384]{1,0:T(8,128)(2,1)S(1)} %get-tuple-element.12), channel_id=1, source_target_pairs={{0,1},{1,0},{2,3},{3,2},{4,12},{5,13},{6,14},{7,15},{8,9},{9,8},{1... | collective-permute-start | bytes 221192 | tf_op jit(solution)/shard_map/ppermute | solution.py:103
  7.5 2.5 %collective-permute-start.5 = (bf16[96,384]{1,0:T(8,128)(2,1)S(1)}, bf16[96,384]{1,0:T(8,128)(2,1)S(1)}, u32[]{:S(2)}, u32[]{:S(2)}) collective-permute-start(bf16[96,384]{1,0:T(8,128)(2,1)S(1)} %get-tuple-element.12), channel_id=1, source_target_pairs={{0,3},{1,2},{2,1},{3,0},{4,28},{5,29},{6,30},{7,31},{8,11},{9,10},... | collective-permute-start | bytes 221192 | tf_op jit(solution)/shard_map/ppermute | solution.py:103
  10.0 2.4 %collective-permute-start.4 = (bf16[96,384]{1,0:T(8,128)(2,1)S(1)}, bf16[96,384]{1,0:T(8,128)(2,1)S(1)}, u32[]{:S(2)}, u32[]{:S(2)}) collective-permute-start(bf16[96,384]{1,0:T(8,128)(2,1)S(1)} %get-tuple-element.12), channel_id=1, source_target_pairs={{0,24},{1,25},{2,26},{3,27},{4,7},{5,6},{6,5},{7,4},{8,16},{9,17},... | collective-permute-start | bytes 221192 | tf_op jit(solution)/shard_map/ppermute | solution.py:103
  12.5 0.6 %collective-permute-start.2 = (bf16[96,384]{1,0:T(8,128)(2,1)S(1)}, bf16[96,384]{1,0:T(8,128)(2,1)S(1)}, u32[]{:S(2)}, u32[]{:S(2)}) collective-permute-start(bf16[96,384]{1,0:T(8,128)(2,1)S(1)} %get-tuple-element.12), channel_id=1, source_target_pairs={{0,8},{1,9},{2,10},{3,11},{4,5},{5,4},{6,7},{7,6},{8,0},{9,1},{10,... | collective-permute-start | bytes 221192 | tf_op jit(solution)/shard_map/ppermute | solution.py:103
  13.1 1.5 %collective-permute-done.5 = bf16[96,384]{1,0:T(8,128)(2,1)S(1)} collective-permute-done((bf16[96,384]{1,0:T(8,128)(2,1)S(1)}, bf16[96,384]{1,0:T(8,128)(2,1)S(1)}, u32[]{:S(2)}, u32[]{:S(2)}) %collective-permute-start.5) | collective-permute-done | bytes 73760 | tf_op jit(solution)/shard_map/ppermute | solution.py:103
  14.5 0.1 select_select_fusion
  14.6 2.3 %collective-permute-start.10 = (bf16[96,384]{1,0:T(8,128)(2,1)S(1)}, bf16[96,384]{1,0:T(8,128)(2,1)S(1)}, u32[]{:S(2)}, u32[]{:S(2)}) collective-permute-start(bf16[96,384]{1,0:T(8,128)(2,1)S(1)} %get-tuple-element.6), channel_id=1, source_target_pairs={{0,24},{1,6},{2,26},{3,4},{4,7},{5,25},{6,5},{7,27},{8,15},{9,17},... | collective-permute-start | bytes 221192 | tf_op jit(solution)/shard_map/ppermute | solution.py:103
  16.9 0.6 %collective-permute-start.8 = (bf16[96,384]{1,0:T(8,128)(2,1)S(1)}, bf16[96,384]{1,0:T(8,128)(2,1)S(1)}, u32[]{:S(2)}, u32[]{:S(2)}) collective-permute-start(bf16[96,384]{1,0:T(8,128)(2,1)S(1)} %get-tuple-element.8), channel_id=1, source_target_pairs={{0,8},{1,4},{2,10},{3,6},{4,5},{5,9},{6,7},{7,11},{8,13},{9,1},{10... | collective-permute-start | bytes 221192 | tf_op jit(solution)/shard_map/ppermute | solution.py:103
  17.5 2.1 %collective-permute-start.13 = (bf16[96,384]{1,0:T(8,128)(2,1)S(1)}, bf16[96,384]{1,0:T(8,128)(2,1)S(1)}, u32[]{:S(2)}, u32[]{:S(2)}) collective-permute-start(bf16[96,384]{1,0:T(8,128)(2,1)S(1)} %get-tuple-element.5), channel_id=1, source_target_pairs={{0,4},{1,5},{2,6},{3,7},{4,0},{5,1},{6,2},{7,3},{8,12},{9,13},{10,... | collective-permute-start | bytes 221192 | tf_op jit(solution)/shard_map/ppermute | solution.py:103
  19.7 0.1 collective-permute-start.11
  19.8 0.9 %collective-permute-done.9.refs_4_ = bf16[96,384]{1,0:T(8,128)(2,1)S(1)} collective-permute-done((bf16[96,384]{1,0:T(8,128)(2,1)S(1)}, bf16[96,384]{1,0:T(8,128)(2,1)S(1)}, u32[]{:S(2)}, u32[]{:S(2)}) %collective-permute-start.9) | collective-permute-done | bytes 73760 | tf_op jit(solution)/shard_map/ppermute | solution.py:103
  20.7 0.0 collective-permute-done.8.refs_3_
  20.7 1.0 %collective-permute-start.12 = (bf16[288,384]{1,0:T(8,128)(2,1)S(1)}, bf16[288,384]{1,0:T(8,128)(2,1)S(1)}, u32[]{:S(2)}, u32[]{:S(2)}) collective-permute-start(bf16[288,384]{1,0:T(8,128)(2,1)S(1)} %pad_maximum_fusion.1), channel_id=1, source_target_pairs={{0,4},{1,5},{2,6},{3,7},{4,0},{5,1},{6,2},{7,3},{8,12},{9,13},{10,... | collective-permute-start | bytes 663560 | tf_op jit(solution)/shard_map/ppermute | solution.py:103
  21.7 1.1 %collective-permute-done.12.refs_7_ = bf16[288,384]{1,0:T(8,128)(2,1)S(1)} collective-permute-done((bf16[288,384]{1,0:T(8,128)(2,1)S(1)}, bf16[288,384]{1,0:T(8,128)(2,1)S(1)}, u32[]{:S(2)}, u32[]{:S(2)}) %collective-permute-start.12) | collective-permute-done | bytes 221216 | tf_op jit(solution)/shard_map/ppermute | solution.py:103
  22.8 1.5 %finish.1 = f32[384,768]{1,0:T(8,128)} custom-call(bf16[96,384]{1,0:T(8,128)(2,1)S(1)} %collective-permute-done.2.refs_0_, bf16[96,384]{1,0:T(8,128)(2,1)S(1)} %collective-permute-done.3.refs_1_, bf16[96,384]{1,0:T(8,128)(2,1)S(1)} %collective-permute-done.4.refs_2_, bf16[96,384]{1,0:T(8,128)(2,1)S(1)} %collective-permute-done.8.refs_3_, ...), custom_call_target="tpu_custom_call" | custom-call | tf_op jit(solution)/shard_map/finish/pallas_call | solution.py:153
  (17 shorter events, 0.2 us)
Async XLA Ops:
  0.0 2.0 %collective-permute-start.1 = (bf16[48,384]{1,0:T(8,128)(2,1)}, bf16[48,384]{1,0:T(8,128)(2,1)S(1)}, u32[]{:S(2)}, u32[]{:S(2)}) collective-permute-start(bf16[48,384]{1,0:T(8,128)(2,1)} %bitcast.3), channel_id=1, source_target_pairs={{0,4},{1,5},{2,6},{3,7},{4,0},{5,1},{6,2},{7,3},{8,12},{9,13},{10,... | collective-permute-start | bytes 110600 | tf_op jit(solution)/shard_map/ppermute | solution.py:103
  0.5 1.6 %collective-permute-start = (bf16[24,768]{1,0:T(8,128)(2,1)}, bf16[24,768]{1,0:T(8,128)(2,1)S(1)}, u32[]{:S(2)}, u32[]{:S(2)}) collective-permute-start(bf16[24,768]{1,0:T(8,128)(2,1)} %param.4), channel_id=1, source_target_pairs={{0,4},{1,5},{2,6},{3,7},{4,0},{5,1},{6,2},{7,3},{8,12},{9,13},{10,... | collective-permute-start | bytes 110600 | tf_op jit(solution)/shard_map/ppermute | solution.py:103
  2.1 20.7 %copy-start = (f32[3072]{0:T(1024)S(1)}, f32[3072]{0:T(1024)}, u32[]{:S(2)}) copy-start(f32[3072]{0:T(1024)} %param.5) | copy-start | bytes 36868
  2.1 10.3 %collective-permute-start.6 = (bf16[96,384]{1,0:T(8,128)(2,1)S(1)}, bf16[96,384]{1,0:T(8,128)(2,1)S(1)}, u32[]{:S(2)}, u32[]{:S(2)}) collective-permute-start(bf16[96,384]{1,0:T(8,128)(2,1)S(1)} %get-tuple-element.11), channel_id=1, source_target_pairs={{0,16},{1,17},{2,18},{3,19},{4,6},{5,7},{6,4},{7,5},{8,24},{9,25},... | collective-permute-start | bytes 221192 | tf_op jit(solution)/shard_map/ppermute | solution.py:103
  5.2 11.7 %collective-permute-start.3 = (bf16[96,384]{1,0:T(8,128)(2,1)S(1)}, bf16[96,384]{1,0:T(8,128)(2,1)S(1)}, u32[]{:S(2)}, u32[]{:S(2)}) collective-permute-start(bf16[96,384]{1,0:T(8,128)(2,1)S(1)} %get-tuple-element.11), channel_id=1, source_target_pairs={{0,6},{1,7},{2,4},{3,5},{4,16},{5,17},{6,18},{7,19},{8,14},{9,15},... | collective-permute-start | bytes 221192 | tf_op jit(solution)/shard_map/ppermute | solution.py:103
  5.9 7.1 %collective-permute-start.7 = (bf16[96,384]{1,0:T(8,128)(2,1)S(1)}, bf16[96,384]{1,0:T(8,128)(2,1)S(1)}, u32[]{:S(2)}, u32[]{:S(2)}) collective-permute-start(bf16[96,384]{1,0:T(8,128)(2,1)S(1)} %get-tuple-element.12), channel_id=1, source_target_pairs={{0,1},{1,0},{2,3},{3,2},{4,12},{5,13},{6,14},{7,15},{8,9},{9,8},{1... | collective-permute-start | bytes 221192 | tf_op jit(solution)/shard_map/ppermute | solution.py:103
  7.5 7.0 %collective-permute-start.5 = (bf16[96,384]{1,0:T(8,128)(2,1)S(1)}, bf16[96,384]{1,0:T(8,128)(2,1)S(1)}, u32[]{:S(2)}, u32[]{:S(2)}) collective-permute-start(bf16[96,384]{1,0:T(8,128)(2,1)S(1)} %get-tuple-element.12), channel_id=1, source_target_pairs={{0,3},{1,2},{2,1},{3,0},{4,28},{5,29},{6,30},{7,31},{8,11},{9,10},... | collective-permute-start | bytes 221192 | tf_op jit(solution)/shard_map/ppermute | solution.py:103
  10.0 7.6 %collective-permute-start.4 = (bf16[96,384]{1,0:T(8,128)(2,1)S(1)}, bf16[96,384]{1,0:T(8,128)(2,1)S(1)}, u32[]{:S(2)}, u32[]{:S(2)}) collective-permute-start(bf16[96,384]{1,0:T(8,128)(2,1)S(1)} %get-tuple-element.12), channel_id=1, source_target_pairs={{0,24},{1,25},{2,26},{3,27},{4,7},{5,6},{6,5},{7,4},{8,16},{9,17},... | collective-permute-start | bytes 221192 | tf_op jit(solution)/shard_map/ppermute | solution.py:103
  12.5 7.2 %collective-permute-start.2 = (bf16[96,384]{1,0:T(8,128)(2,1)S(1)}, bf16[96,384]{1,0:T(8,128)(2,1)S(1)}, u32[]{:S(2)}, u32[]{:S(2)}) collective-permute-start(bf16[96,384]{1,0:T(8,128)(2,1)S(1)} %get-tuple-element.12), channel_id=1, source_target_pairs={{0,8},{1,9},{2,10},{3,11},{4,5},{5,4},{6,7},{7,6},{8,0},{9,1},{10,... | collective-permute-start | bytes 221192 | tf_op jit(solution)/shard_map/ppermute | solution.py:103
  14.6 5.2 %collective-permute-start.10 = (bf16[96,384]{1,0:T(8,128)(2,1)S(1)}, bf16[96,384]{1,0:T(8,128)(2,1)S(1)}, u32[]{:S(2)}, u32[]{:S(2)}) collective-permute-start(bf16[96,384]{1,0:T(8,128)(2,1)S(1)} %get-tuple-element.6), channel_id=1, source_target_pairs={{0,24},{1,6},{2,26},{3,4},{4,7},{5,25},{6,5},{7,27},{8,15},{9,17},... | collective-permute-start | bytes 221192 | tf_op jit(solution)/shard_map/ppermute | solution.py:103
  16.9 3.8 %collective-permute-start.9 = (bf16[96,384]{1,0:T(8,128)(2,1)S(1)}, bf16[96,384]{1,0:T(8,128)(2,1)S(1)}, u32[]{:S(2)}, u32[]{:S(2)}) collective-permute-start(bf16[96,384]{1,0:T(8,128)(2,1)S(1)} %get-tuple-element.7), channel_id=1, source_target_pairs={{0,6},{1,17},{2,4},{3,19},{4,16},{5,7},{6,18},{7,5},{8,24},{9,15},... | collective-permute-start | bytes 221192 | tf_op jit(solution)/shard_map/ppermute | solution.py:103
  16.9 3.8 %collective-permute-start.8 = (bf16[96,384]{1,0:T(8,128)(2,1)S(1)}, bf16[96,384]{1,0:T(8,128)(2,1)S(1)}, u32[]{:S(2)}, u32[]{:S(2)}) collective-permute-start(bf16[96,384]{1,0:T(8,128)(2,1)S(1)} %get-tuple-element.8), channel_id=1, source_target_pairs={{0,8},{1,4},{2,10},{3,6},{4,5},{5,9},{6,7},{7,11},{8,13},{9,1},{10... | collective-permute-start | bytes 221192 | tf_op jit(solution)/shard_map/ppermute | solution.py:103
  17.5 4.1 %collective-permute-start.13 = (bf16[96,384]{1,0:T(8,128)(2,1)S(1)}, bf16[96,384]{1,0:T(8,128)(2,1)S(1)}, u32[]{:S(2)}, u32[]{:S(2)}) collective-permute-start(bf16[96,384]{1,0:T(8,128)(2,1)S(1)} %get-tuple-element.5), channel_id=1, source_target_pairs={{0,4},{1,5},{2,6},{3,7},{4,0},{5,1},{6,2},{7,3},{8,12},{9,13},{10,... | collective-permute-start | bytes 221192 | tf_op jit(solution)/shard_map/ppermute | solution.py:103
  19.7 2.0 %collective-permute-start.11 = (bf16[288,384]{1,0:T(8,128)(2,1)S(1)}, bf16[288,384]{1,0:T(8,128)(2,1)S(1)}, u32[]{:S(2)}, u32[]{:S(2)}) collective-permute-start(bf16[288,384]{1,0:T(8,128)(2,1)S(1)} %pad_maximum_fusion), channel_id=1, source_target_pairs={{0,4},{1,5},{2,6},{3,7},{4,0},{5,1},{6,2},{7,3},{8,12},{9,13},{10,... | collective-permute-start | bytes 663560 | tf_op jit(solution)/shard_map/ppermute | solution.py:103
  20.7 2.1 %collective-permute-start.12 = (bf16[288,384]{1,0:T(8,128)(2,1)S(1)}, bf16[288,384]{1,0:T(8,128)(2,1)S(1)}, u32[]{:S(2)}, u32[]{:S(2)}) collective-permute-start(bf16[288,384]{1,0:T(8,128)(2,1)S(1)} %pad_maximum_fusion.1), channel_id=1, source_target_pairs={{0,4},{1,5},{2,6},{3,7},{4,0},{5,1},{6,2},{7,3},{8,12},{9,13},{10,... | collective-permute-start | bytes 663560 | tf_op jit(solution)/shard_map/ppermute | solution.py:103

commit v4 on v3

v4 whole, which is shorter than its diff:
```python
import functools

import jax
import jax.numpy as jnp
from jax import lax
from jax.experimental import pallas as pl
from jax.experimental.pallas import tpu as pltpu
from jax.sharding import PartitionSpec as P


AXES = ("row", "col")
TILE = 128
SPLIT = 2
VMEM_LIMIT = 12 * 2**20
OVER_FIRST = (((0,), (0,)), ((), ()))


def pick(index, pieces):
    return functools.reduce(
        lambda kept, i: jnp.where(index == i, pieces[i], kept),
        range(1, len(pieces)),
        pieces[0],
    )


def place():
    row, col = lax.axis_index("row"), lax.axis_index("col")
    return row // 2, row % 2, (row // 2) ^ col


def on_core(core, action):
    for h in range(2):
        pl.when(core == h)(functools.partial(action, h))


def load(*refs):
    count = len(refs) // 2
    copies = [
        pltpu.make_async_copy(refs[i], refs[count + i], refs[-1].at[i]) for i in range(count)
    ]
    for copy in copies:
        copy.start()
    for copy in copies:
        copy.wait()


def pack(kp, ka, rt, their_i, their_a, my_i, my_a, *packs):
    _, core, _ = place()

    def fill(h):
        for owner, i, a in ((h, my_i, my_a), (1 - h, their_i, their_a)):
            packs[1 - h][owner * kp : (owner + 1) * kp, :] = i[...]
            for half in range(2):
                low = half * kp + owner * ka
                packs[h][low : low + ka, :] = a[:, half * rt : (half + 1) * rt]

    on_core(core, fill)


def prepare(n, kp, rt, *refs):
    direct, swap, energy, packs = refs[: n - 1], refs[n - 1], refs[n], refs[n + 1 : n + 3]
    ladder, scale, lhs, rhs = refs[n + 3 :]
    chip, core, shift = place()

    def gather(h):
        for j in range(n):
            here, moved = pl.ds(j * kp, kp), pl.ds(pl.multiple_of((shift ^ j) * kp, kp), kp)
            if j == 0:
                i, a = packs[1 - h], packs[h]
                i_at, a_at = h * kp, 0
            else:
                mine, gift = (direct[j - 1], 0), (swap, 2 * kp * (j - 1))
                (i, i_at), (a, a_at) = (gift, mine) if h == 0 else (mine, gift)
                i_at += h * kp
            lhs[moved, :] = i[i_at : i_at + kp, :]
            rhs[here, :rt] = a[a_at : a_at + kp, :]
            rhs[here, rt:] = a[a_at + kp : a_at + 2 * kp, :]

    on_core(core, gather)
    row_start = (2 * chip + core) * rt
    col_start = (chip ^ shift) * 2 * rt
    across = energy[:, pl.ds(pl.multiple_of(col_start, 2 * rt), 2 * rt)]
    for i in range(rt // TILE):
        rows = slice(i * TILE, (i + 1) * TILE)
        ladder[rows, :] = lax.dot_general(
            lhs[:, rows], rhs[...], OVER_FIRST, preferred_element_type=jnp.float32
        )
        along = energy[:, pl.ds(pl.multiple_of(row_start + i * TILE, TILE), TILE)]
        down = jnp.broadcast_to(along, (TILE, TILE)).T[:, :1]
        scale[rows, :] = 1.0 / (down + across)


def finish(n, kp, rt, *refs):
    settled, swap, near_i, near_a = refs[: n - 1], refs[n - 1], refs[n], refs[n + 1]
    ladder, scale, out, lhs, rhs, buffer, done = refs[n + 2 :]
    _, core, shift = place()

    def gather(h):
        for j in range(n):
            here, moved = pl.ds(j * kp, kp), pl.ds(pl.multiple_of((shift ^ j) * kp, kp), kp)
            if j == 0:
                (i, i_at), (a, a_at) = (near_i, 0), (near_a, 0)
            else:
                mine, gift = (settled[j - 1], 0), (swap, 2 * kp * (j - 1))
                (i, i_at), (a, a_at) = (gift, mine) if h == 0 else (mine, gift)
            a_at += h * kp
            lhs[here, :] = a[a_at : a_at + kp, :]
            rhs[moved, :rt] = i[i_at : i_at + kp, :]
            rhs[moved, rt:] = i[i_at + kp : i_at + 2 * kp, :]

    on_core(core, gather)
    copies = []
    for i in range(rt // TILE):
        rows = slice(i * TILE, (i + 1) * TILE)
        partner = lax.dot_general(
            lhs[:, rows], rhs[...], OVER_FIRST, preferred_element_type=jnp.float32
        )
        partner = partner.astype(jnp.bfloat16).astype(jnp.float32)
        for part in range(SPLIT):
            size = TILE // SPLIT
            low = i * TILE + part * size
            some = slice(low, low + size)
            rounded = partner[part * size : (part + 1) * size]
            buffer[some, :] = (ladder[some, :] + rounded) * scale[some, :]
            sem = done.at[i * SPLIT + part]
            copies.append(pltpu.make_async_copy(buffer.at[some], out.at[some], sem))
            copies[-1].start()
    for copy in copies:
        copy.wait()


def call(kernel, inputs, placed, out_specs, out_shape, scratch):
    keep = pl.BlockSpec(memory_space=pltpu.VMEM)
    return pl.pallas_call(
        kernel,
        in_specs=[keep] * (len(inputs) + len(placed)),
        out_specs=out_specs,
        out_shape=out_shape,
        scratch_shapes=scratch,
        compiler_params=pltpu.CompilerParams(vmem_limit_bytes=VMEM_LIMIT),
    )(*[pltpu.with_memory_space_constraint(x, pltpu.VMEM) for x in [*inputs, *placed]])


def paired(integrals, amplitudes, energies):
    n = lax.axis_size("col")
    rt, kp = integrals.shape
    ka = amplitudes.shape[0]
    _, core, shift = place()
    first = core == 0

    def send(value, target):
        pairs = [
            ((2 * k + h) * n + c, (2 * tk + th) * n + tc)
            for k in range(n)
            for h in range(2)
            for c in range(n)
            for tk, th, tc in [target(k, h, c)]
        ]
        return lax.ppermute(value, AXES, pairs)

    def other(k, h, c):
        return k, 1 - h, c

    def carrier(j):
        return 1 - j % 2

    their_i, their_a = send(integrals.T, other), send(amplitudes, other)
    keep = pl.BlockSpec(memory_space=pltpu.VMEM)
    mine = (integrals.T, amplitudes)
    mine = pl.pallas_call(
        load,
        in_specs=[pl.BlockSpec(memory_space=pltpu.HBM)] * 2,
        out_specs=[keep] * 2,
        out_shape=[pltpu.VMEM(x.shape, x.dtype) for x in mine],
        scratch_shapes=[pltpu.SemaphoreType.DMA((2,))],
        compiler_params=pltpu.CompilerParams(vmem_limit_bytes=VMEM_LIMIT),
        name="load",
    )(*[pltpu.with_memory_space_constraint(x, pltpu.HBM) for x in mine])
    own = call(
        functools.partial(pack, kp, ka, rt),
        [their_i, their_a],
        mine,
        [keep] * 2,
        [pltpu.VMEM((2 * kp, rt), jnp.bfloat16)] * 2,
        [],
    )
    order = range(n - 1, 0, -1)
    gathered, direct, settled = {0: own[carrier(0)]}, {}, {}
    for j in order:
        gathered[j] = send(
            own[carrier(j)], lambda k, h, c: (k, h, c ^ j) if h == carrier(j) else (k ^ j, h, c)
        )
    for j in order:
        direct[j] = send(
            own[carrier(j)], lambda k, h, c: (k ^ j, 0, c) if h == carrier(j) else (k, 1, c ^ j)
        )
    for j in order:
        settled[j] = send(
            pick(shift ^ j, gathered),
            lambda k, h, c: (k ^ j, 0, c) if h == carrier(k ^ c ^ j) else (k, 1, c ^ j),
        )
    near = pick(shift, gathered)
    far = send(near, other)
    has_a = functools.reduce(
        lambda kept, m: jnp.where(shift == m, core == carrier(m), kept), range(n), first
    )
    near_a, near_i = jnp.where(has_a, near, far), jnp.where(has_a, far, near)
    direct, settled = [[x[j] for j in range(1, n)] for x in (direct, settled)]
    swap_d, swap_s = send(jnp.concatenate(direct), other), send(jnp.concatenate(settled), other)
    early = call(
        functools.partial(prepare, n, kp, rt),
        [*direct, swap_d, energies.reshape(1, -1)],
        own,
        [keep] * 2,
        [pltpu.VMEM((rt, 2 * rt), jnp.float32)] * 2,
        [pltpu.VMEM((n * kp, width), jnp.bfloat16) for width in (rt, 2 * rt)],
    )
    return call(
        functools.partial(finish, n, kp, rt),
        [*settled, swap_s, near_i, near_a],
        early,
        pl.BlockSpec(memory_space=pl.ANY),
        jax.ShapeDtypeStruct((rt, 2 * rt), jnp.float32),
        [
            *[pltpu.VMEM((n * kp, width), jnp.bfloat16) for width in (rt, 2 * rt)],
            pltpu.VMEM((rt, 2 * rt), jnp.float32),
            pltpu.SemaphoreType.DMA((rt // TILE * SPLIT,)),
        ],
    )


def general(integrals, amplitudes, energies):
    rows_tile = integrals.shape[0]
    cols_tile = amplitudes.shape[1]
    n_row = lax.axis_size("row")
    n_col = lax.axis_size("col")
    block = rows_tile // n_col
    panel = lax.all_gather(integrals, "col", axis=1, tiled=True)
    ladder = jnp.dot(
        panel,
        lax.all_gather(amplitudes, "row", axis=0, tiled=True),
        preferred_element_type=jnp.float32,
    )
    rounded = ladder.astype(jnp.bfloat16)
    by_rows = lax.all_to_all(rounded, "col", split_axis=0, concat_axis=1, tiled=True)
    lifted = lax.all_to_all(by_rows, "row", split_axis=1, concat_axis=0, tiled=True)
    shaped = lifted.reshape(n_row, 1, block, n_col * block)
    settled = lax.all_to_all(shaped, "col", split_axis=0, concat_axis=1, tiled=True)
    partner = settled.reshape(n_row * block, n_col * block).T.astype(jnp.float32)
    row_start = lax.axis_index("row") * rows_tile
    col_start = lax.axis_index("col") * cols_tile
    row_energy = lax.dynamic_slice_in_dim(energies, row_start, rows_tile, 0)
    col_energy = lax.dynamic_slice_in_dim(energies, col_start, cols_tile, 0)
    return (ladder + partner) / (row_energy[:, None] + col_energy[None, :])


def body(integrals, amplitudes, energies):
    rt, kp = integrals.shape
    n_row, n_col = lax.axis_size("row"), lax.axis_size("col")
    fits = (
        n_row == 2 * n_col
        and n_col & (n_col - 1) == 0
        and amplitudes.shape == (kp // 2, 2 * rt)
        and rt % 128 == 0
        and kp % 16 == 0
    )
    return (paired if fits else general)(integrals, amplitudes, energies)


def solution(mesh):
    placed = (P("row", "col"), P("row", "col"), P())
    return jax.shard_map(
        body, mesh=mesh, in_specs=placed, out_specs=P("row", "col"), check_vma=False
    )
```

time: 24.5 us -> 22.5 us (0.918)
  starting transfers between devices: 17.5 us -> 14.8 us
  Pallas kernels: 1.45 us -> 2.63 us
  waiting for transfers between devices: 3.44 us -> 4.61 us
  other arithmetic: 0.98 us -> 0.13 us
  local copies, waits for them, and re-layouts: 0.75 us -> 0.01 us
    ppermute x14, starting transfers between devices: 17.5 us -> 14.8 us  [send(): return lax.ppermute(value, AXES, pairs)]
    pallas_call x1 -> x4, Pallas kernels: 1.45 us -> 2.63 us  [the longest x3 1.83 us: call(): pl.pallas_call(kernel, in_specs=[keep] * (len(inputs) + len(placed)), out...]
    ppermute x14, waiting for transfers between devices: 3.44 us -> 4.61 us  [send(): return lax.ppermute(value, AXES, pairs)]
    concatenate x2 -> x0, other arithmetic: 0.78 us -> none  [the longest x1 0.78 us: paired(): jnp.concatenate([integrals.T, amplitudes[:, :rt], amplitudes[:, rt:]])]
    slice x1 -> x0, local copies, waits for them, and re-layouts: 0.74 us -> none  [paired(): amplitudes[:, :rt]]
  transfers between devices with their start and end apart: 14 -> 14, of which waited for: 3 -> 7; matrix products, arithmetic and copies ran while one was open for 7% -> 1% of each run, Pallas kernels for 0% -> 6%
where the time goes in v4:
time: 22.5 us; the launch traced here: 22.2 us
  starting transfers between devices  14.8 us (66%)
  waiting for transfers between devices  4.61 us (20%)
  Pallas kernels  2.63 us (12%)
    ppermute x14, starting transfers between devices, send(): return lax.ppermute(value, AXES, pairs)  14.8 us
    ppermute x14, waiting for transfers between devices, send(): return lax.ppermute(value, AXES, pairs)  4.61 us
    pallas_call x3, Pallas kernels, call(): pl.pallas_call(kernel, in_specs=[keep] * (len(inputs) + len(placed)), out...  1.83 us
    pallas_call x1, Pallas kernels, paired(): pl.pallas_call(load, in_specs=[pl.BlockSpec(memory_space=pltpu.HBM)] * 2,...  0.8 us
  transfers between devices with their start and end apart: 14, of which 7 were waited for; matrix products, arithmetic and copies ran while one was open for 1% of the time, Pallas kernels for 6%

profile of v4, /device:TPU:0, one launch (start us, length us, event | category | flops | bytes accessed | tf_op | source)
XLA Modules:
  0.0 22.2 jit_solution(7313634762043115052)
XLA Ops:
  0.0 0.5 %collective-permute-start = (bf16[48,384]{1,0:T(8,128)(2,1)}, bf16[48,384]{1,0:T(8,128)(2,1)S(1)}, u32[]{:S(2)}, u32[]{:S(2)}) collective-permute-start(bf16[48,384]{1,0:T(8,128)(2,1)} %bitcast.3), channel_id=1, source_target_pairs={{0,4},{1,5},{2,6},{3,7},{4,0},{5,1},{6,2},{7,3},{8,12},{9,13},{10,... | collective-permute-start | bytes 110600 | tf_op jit(solution)/shard_map/ppermute | solution.py:159
  0.5 0.1 collective-permute-start.1
  0.6 0.8 %load.1 = (bf16[48,384]{1,0:T(8,128)(2,1)S(1)}, bf16[24,768]{1,0:T(8,128)(2,1)S(1)}) custom-call(bf16[48,384]{1,0:T(8,128)(2,1)} %bitcast.4, bf16[24,768]{1,0:T(8,128)(2,1)} %refs_1_.1), custom_call_target="tpu_custom_call" | custom-call | tf_op jit(solution)/shard_map/load/pallas_call | solution.py:170
  1.4 0.2 collective-permute-done.their_i
  1.6 0.3 %collective-permute-done.1.their_a = bf16[24,768]{1,0:T(8,128)(2,1)S(1)} collective-permute-done((bf16[24,768]{1,0:T(8,128)(2,1)}, bf16[24,768]{1,0:T(8,128)(2,1)S(1)}, u32[]{:S(2)}, u32[]{:S(2)}) %collective-permute-start.1) | collective-permute-done | bytes 36896 | tf_op jit(solution)/shard_map/ppermute | solution.py:159
  1.9 2.7 %collective-permute-start.3 = (bf16[96,384]{1,0:T(8,128)(2,1)S(1)}, bf16[96,384]{1,0:T(8,128)(2,1)S(1)}, u32[]{:S(2)}, u32[]{:S(2)}) collective-permute-start(bf16[96,384]{1,0:T(8,128)(2,1)S(1)} %get-tuple-element.14.refs_6_), channel_id=1, source_target_pairs={{0,16},{1,17},{2,18},{3,19},{4,6},{5,7},{6,4},{7,5},{8,24},{9,25},... | collective-permute-start | bytes 221192 | tf_op jit(solution)/shard_map/ppermute | solution.py:159
  4.7 1.6 %collective-permute-start.4 = (bf16[96,384]{1,0:T(8,128)(2,1)S(1)}, bf16[96,384]{1,0:T(8,128)(2,1)S(1)}, u32[]{:S(2)}, u32[]{:S(2)}) collective-permute-start(bf16[96,384]{1,0:T(8,128)(2,1)S(1)} %get-tuple-element.13.refs_5_), channel_id=1, source_target_pairs={{0,1},{1,0},{2,3},{3,2},{4,12},{5,13},{6,14},{7,15},{8,9},{9,8},{1... | collective-permute-start | bytes 221192 | tf_op jit(solution)/shard_map/ppermute | solution.py:159
  6.3 2.5 %collective-permute-start.2 = (bf16[96,384]{1,0:T(8,128)(2,1)S(1)}, bf16[96,384]{1,0:T(8,128)(2,1)S(1)}, u32[]{:S(2)}, u32[]{:S(2)}) collective-permute-start(bf16[96,384]{1,0:T(8,128)(2,1)S(1)} %get-tuple-element.13.refs_5_), channel_id=1, source_target_pairs={{0,3},{1,2},{2,1},{3,0},{4,28},{5,29},{6,30},{7,31},{8,11},{9,10},... | collective-permute-start | bytes 221192 | tf_op jit(solution)/shard_map/ppermute | solution.py:159
  8.7 1.4 %collective-permute-start.12 = (bf16[96,384]{1,0:T(8,128)(2,1)S(1)}, bf16[96,384]{1,0:T(8,128)(2,1)S(1)}, u32[]{:S(2)}, u32[]{:S(2)}) collective-permute-start(bf16[96,384]{1,0:T(8,128)(2,1)S(1)} %get-tuple-element.13.refs_5_), channel_id=1, source_target_pairs={{0,24},{1,25},{2,26},{3,27},{4,7},{5,6},{6,5},{7,4},{8,16},{9,17},... | collective-permute-start | bytes 221192 | tf_op jit(solution)/shard_map/ppermute | solution.py:159
  10.2 0.0 collective-permute-done.3
  10.2 0.5 %collective-permute-start.10 = (bf16[96,384]{1,0:T(8,128)(2,1)S(1)}, bf16[96,384]{1,0:T(8,128)(2,1)S(1)}, u32[]{:S(2)}, u32[]{:S(2)}) collective-permute-start(bf16[96,384]{1,0:T(8,128)(2,1)S(1)} %get-tuple-element.13.refs_5_), channel_id=1, source_target_pairs={{0,8},{1,9},{2,10},{3,11},{4,5},{5,4},{6,7},{7,6},{8,0},{9,1},{10,... | collective-permute-start | bytes 221192 | tf_op jit(solution)/shard_map/ppermute | solution.py:159
  10.7 1.7 %collective-permute-done.2 = bf16[96,384]{1,0:T(8,128)(2,1)S(1)} collective-permute-done((bf16[96,384]{1,0:T(8,128)(2,1)S(1)}, bf16[96,384]{1,0:T(8,128)(2,1)S(1)}, u32[]{:S(2)}, u32[]{:S(2)}) %collective-permute-start.2) | collective-permute-done | bytes 73760 | tf_op jit(solution)/shard_map/ppermute | solution.py:159
  12.4 0.1 select_select_fusion
  12.5 1.5 %collective-permute-start.7 = (bf16[96,384]{1,0:T(8,128)(2,1)S(1)}, bf16[96,384]{1,0:T(8,128)(2,1)S(1)}, u32[]{:S(2)}, u32[]{:S(2)}) collective-permute-start(bf16[96,384]{1,0:T(8,128)(2,1)S(1)} %get-tuple-element.18), channel_id=1, source_target_pairs={{0,24},{1,6},{2,26},{3,4},{4,7},{5,25},{6,5},{7,27},{8,15},{9,17},... | collective-permute-start | bytes 221192 | tf_op jit(solution)/shard_map/ppermute | solution.py:159
  14.0 1.7 %collective-permute-start.5 = (bf16[96,384]{1,0:T(8,128)(2,1)S(1)}, bf16[96,384]{1,0:T(8,128)(2,1)S(1)}, u32[]{:S(2)}, u32[]{:S(2)}) collective-permute-start(bf16[96,384]{1,0:T(8,128)(2,1)S(1)} %get-tuple-element.20), channel_id=1, source_target_pairs={{0,8},{1,4},{2,10},{3,6},{4,5},{5,9},{6,7},{7,11},{8,13},{9,1},{10... | collective-permute-start | bytes 221192 | tf_op jit(solution)/shard_map/ppermute | solution.py:159
  15.7 1.0 %collective-permute-start.9 = (bf16[96,384]{1,0:T(8,128)(2,1)S(1)}, bf16[96,384]{1,0:T(8,128)(2,1)S(1)}, u32[]{:S(2)}, u32[]{:S(2)}) collective-permute-start(bf16[96,384]{1,0:T(8,128)(2,1)S(1)} %get-tuple-element.17), channel_id=1, source_target_pairs={{0,4},{1,5},{2,6},{3,7},{4,0},{5,1},{6,2},{7,3},{8,12},{9,13},{10,... | collective-permute-start | bytes 221192 | tf_op jit(solution)/shard_map/ppermute | solution.py:159
  16.7 0.1 collective-permute-start.13
  16.8 0.5 %collective-permute-done.7.refs_2_ = bf16[96,384]{1,0:T(8,128)(2,1)S(1)} collective-permute-done((bf16[96,384]{1,0:T(8,128)(2,1)S(1)}, bf16[96,384]{1,0:T(8,128)(2,1)S(1)}, u32[]{:S(2)}, u32[]{:S(2)}) %collective-permute-start.7) | collective-permute-done | bytes 73760 | tf_op jit(solution)/shard_map/ppermute | solution.py:159
  17.3 0.8 %collective-permute-done.6.refs_1_ = bf16[96,384]{1,0:T(8,128)(2,1)S(1)} collective-permute-done((bf16[96,384]{1,0:T(8,128)(2,1)S(1)}, bf16[96,384]{1,0:T(8,128)(2,1)S(1)}, u32[]{:S(2)}, u32[]{:S(2)}) %collective-permute-start.6) | collective-permute-done | bytes 73760 | tf_op jit(solution)/shard_map/ppermute | solution.py:159
  18.0 0.5 %collective-permute-done.5.refs_0_ = bf16[96,384]{1,0:T(8,128)(2,1)S(1)} collective-permute-done((bf16[96,384]{1,0:T(8,128)(2,1)S(1)}, bf16[96,384]{1,0:T(8,128)(2,1)S(1)}, u32[]{:S(2)}, u32[]{:S(2)}) %collective-permute-start.5) | collective-permute-done | bytes 73760 | tf_op jit(solution)/shard_map/ppermute | solution.py:159
  18.5 1.2 %collective-permute-start.8 = (bf16[288,384]{1,0:T(8,128)(2,1)S(1)}, bf16[288,384]{1,0:T(8,128)(2,1)S(1)}, u32[]{:S(2)}, u32[]{:S(2)}) collective-permute-start(bf16[288,384]{1,0:T(8,128)(2,1)S(1)} %pad_maximum_fusion), channel_id=1, source_target_pairs={{0,4},{1,5},{2,6},{3,7},{4,0},{5,1},{6,2},{7,3},{8,12},{9,13},{10,... | collective-permute-start | bytes 663560 | tf_op jit(solution)/shard_map/ppermute | solution.py:159
  19.8 0.5 %shard_map.38 = (f32[384,768]{1,0:T(8,128)S(1)}, f32[384,768]{1,0:T(8,128)S(1)}) custom-call(bf16[96,384]{1,0:T(8,128)(2,1)S(1)} %collective-permute-done.10.refs_0_, bf16[96,384]{1,0:T(8,128)(2,1)S(1)} %collective-permute-done.11.refs_1_, bf16[96,384]{1,0:T(8,128)(2,1)S(1)} %collective-permute-done.12.refs_2_, ...), custom_call_target="tpu_custom_call" | custom-call | tf_op jit(solution)/shard_map/pallas_call | solution.py:134
  20.3 0.6 %collective-permute-done.8.refs_3_ = bf16[288,384]{1,0:T(8,128)(2,1)S(1)} collective-permute-done((bf16[288,384]{1,0:T(8,128)(2,1)S(1)}, bf16[288,384]{1,0:T(8,128)(2,1)S(1)}, u32[]{:S(2)}, u32[]{:S(2)}) %collective-permute-start.8) | collective-permute-done | bytes 221216 | tf_op jit(solution)/shard_map/ppermute | solution.py:159
  20.9 1.3 %shard_map.39 = f32[384,768]{1,0:T(8,128)} custom-call(bf16[96,384]{1,0:T(8,128)(2,1)S(1)} %collective-permute-done.5.refs_0_, bf16[96,384]{1,0:T(8,128)(2,1)S(1)} %collective-permute-done.6.refs_1_, bf16[96,384]{1,0:T(8,128)(2,1)S(1)} %collective-permute-done.7.refs_2_, bf16[288,384]{1,0:T(8,128)(2,1)S(1)} %collective-permute-done.8.refs_3_, ...), custom_call_target="tpu_custom_call" | custom-call | tf_op jit(solution)/shard_map/pallas_call | solution.py:134
  (14 shorter events, 0.1 us)
Async XLA Ops:
  0.0 19.8 %copy-start = (f32[3072]{0:T(1024)S(1)}, f32[3072]{0:T(1024)}, u32[]{:S(2)}) copy-start(f32[3072]{0:T(1024)} %param.5) | copy-start | bytes 36868
  0.0 1.6 %collective-permute-start = (bf16[48,384]{1,0:T(8,128)(2,1)}, bf16[48,384]{1,0:T(8,128)(2,1)S(1)}, u32[]{:S(2)}, u32[]{:S(2)}) collective-permute-start(bf16[48,384]{1,0:T(8,128)(2,1)} %bitcast.3), channel_id=1, source_target_pairs={{0,4},{1,5},{2,6},{3,7},{4,0},{5,1},{6,2},{7,3},{8,12},{9,13},{10,... | collective-permute-start | bytes 110600 | tf_op jit(solution)/shard_map/ppermute | solution.py:159
  0.5 1.4 %collective-permute-start.1 = (bf16[24,768]{1,0:T(8,128)(2,1)}, bf16[24,768]{1,0:T(8,128)(2,1)S(1)}, u32[]{:S(2)}, u32[]{:S(2)}) collective-permute-start(bf16[24,768]{1,0:T(8,128)(2,1)} %refs_1_.1), channel_id=1, source_target_pairs={{0,4},{1,5},{2,6},{3,7},{4,0},{5,1},{6,2},{7,3},{8,12},{9,13},{10,... | collective-permute-start | bytes 110600 | tf_op jit(solution)/shard_map/ppermute | solution.py:159
  1.9 8.2 %collective-permute-start.3 = (bf16[96,384]{1,0:T(8,128)(2,1)S(1)}, bf16[96,384]{1,0:T(8,128)(2,1)S(1)}, u32[]{:S(2)}, u32[]{:S(2)}) collective-permute-start(bf16[96,384]{1,0:T(8,128)(2,1)S(1)} %get-tuple-element.14.refs_6_), channel_id=1, source_target_pairs={{0,16},{1,17},{2,18},{3,19},{4,6},{5,7},{6,4},{7,5},{8,24},{9,25},... | collective-permute-start | bytes 221192 | tf_op jit(solution)/shard_map/ppermute | solution.py:159
  4.7 6.0 %collective-permute-start.4 = (bf16[96,384]{1,0:T(8,128)(2,1)S(1)}, bf16[96,384]{1,0:T(8,128)(2,1)S(1)}, u32[]{:S(2)}, u32[]{:S(2)}) collective-permute-start(bf16[96,384]{1,0:T(8,128)(2,1)S(1)} %get-tuple-element.13.refs_5_), channel_id=1, source_target_pairs={{0,1},{1,0},{2,3},{3,2},{4,12},{5,13},{6,14},{7,15},{8,9},{9,8},{1... | collective-permute-start | bytes 221192 | tf_op jit(solution)/shard_map/ppermute | solution.py:159
  6.3 6.2 %collective-permute-start.2 = (bf16[96,384]{1,0:T(8,128)(2,1)S(1)}, bf16[96,384]{1,0:T(8,128)(2,1)S(1)}, u32[]{:S(2)}, u32[]{:S(2)}) collective-permute-start(bf16[96,384]{1,0:T(8,128)(2,1)S(1)} %get-tuple-element.13.refs_5_), channel_id=1, source_target_pairs={{0,3},{1,2},{2,1},{3,0},{4,28},{5,29},{6,30},{7,31},{8,11},{9,10},... | collective-permute-start | bytes 221192 | tf_op jit(solution)/shard_map/ppermute | solution.py:159
  8.7 5.2 %collective-permute-start.11 = (bf16[96,384]{1,0:T(8,128)(2,1)S(1)}, bf16[96,384]{1,0:T(8,128)(2,1)S(1)}, u32[]{:S(2)}, u32[]{:S(2)}) collective-permute-start(bf16[96,384]{1,0:T(8,128)(2,1)S(1)} %get-tuple-element.14.refs_6_), channel_id=1, source_target_pairs={{0,6},{1,7},{2,4},{3,5},{4,16},{5,17},{6,18},{7,19},{8,14},{9,15},... | collective-permute-start | bytes 221192 | tf_op jit(solution)/shard_map/ppermute | solution.py:159
  8.7 6.9 %collective-permute-start.12 = (bf16[96,384]{1,0:T(8,128)(2,1)S(1)}, bf16[96,384]{1,0:T(8,128)(2,1)S(1)}, u32[]{:S(2)}, u32[]{:S(2)}) collective-permute-start(bf16[96,384]{1,0:T(8,128)(2,1)S(1)} %get-tuple-element.13.refs_5_), channel_id=1, source_target_pairs={{0,24},{1,25},{2,26},{3,27},{4,7},{5,6},{6,5},{7,4},{8,16},{9,17},... | collective-permute-start | bytes 221192 | tf_op jit(solution)/shard_map/ppermute | solution.py:159
  10.2 6.5 %collective-permute-start.10 = (bf16[96,384]{1,0:T(8,128)(2,1)S(1)}, bf16[96,384]{1,0:T(8,128)(2,1)S(1)}, u32[]{:S(2)}, u32[]{:S(2)}) collective-permute-start(bf16[96,384]{1,0:T(8,128)(2,1)S(1)} %get-tuple-element.13.refs_5_), channel_id=1, source_target_pairs={{0,8},{1,9},{2,10},{3,11},{4,5},{5,4},{6,7},{7,6},{8,0},{9,1},{10,... | collective-permute-start | bytes 221192 | tf_op jit(solution)/shard_map/ppermute | solution.py:159
  12.5 4.8 %collective-permute-start.7 = (bf16[96,384]{1,0:T(8,128)(2,1)S(1)}, bf16[96,384]{1,0:T(8,128)(2,1)S(1)}, u32[]{:S(2)}, u32[]{:S(2)}) collective-permute-start(bf16[96,384]{1,0:T(8,128)(2,1)S(1)} %get-tuple-element.18), channel_id=1, source_target_pairs={{0,24},{1,6},{2,26},{3,4},{4,7},{5,25},{6,5},{7,27},{8,15},{9,17},... | collective-permute-start | bytes 221192 | tf_op jit(solution)/shard_map/ppermute | solution.py:159
  14.0 4.1 %collective-permute-start.6 = (bf16[96,384]{1,0:T(8,128)(2,1)S(1)}, bf16[96,384]{1,0:T(8,128)(2,1)S(1)}, u32[]{:S(2)}, u32[]{:S(2)}) collective-permute-start(bf16[96,384]{1,0:T(8,128)(2,1)S(1)} %get-tuple-element.19), channel_id=1, source_target_pairs={{0,6},{1,17},{2,4},{3,19},{4,16},{5,7},{6,18},{7,5},{8,24},{9,15},... | collective-permute-start | bytes 221192 | tf_op jit(solution)/shard_map/ppermute | solution.py:159
  14.0 4.5 %collective-permute-start.5 = (bf16[96,384]{1,0:T(8,128)(2,1)S(1)}, bf16[96,384]{1,0:T(8,128)(2,1)S(1)}, u32[]{:S(2)}, u32[]{:S(2)}) collective-permute-start(bf16[96,384]{1,0:T(8,128)(2,1)S(1)} %get-tuple-element.20), channel_id=1, source_target_pairs={{0,8},{1,4},{2,10},{3,6},{4,5},{5,9},{6,7},{7,11},{8,13},{9,1},{10... | collective-permute-start | bytes 221192 | tf_op jit(solution)/shard_map/ppermute | solution.py:159
  15.7 4.1 %collective-permute-start.9 = (bf16[96,384]{1,0:T(8,128)(2,1)S(1)}, bf16[96,384]{1,0:T(8,128)(2,1)S(1)}, u32[]{:S(2)}, u32[]{:S(2)}) collective-permute-start(bf16[96,384]{1,0:T(8,128)(2,1)S(1)} %get-tuple-element.17), channel_id=1, source_target_pairs={{0,4},{1,5},{2,6},{3,7},{4,0},{5,1},{6,2},{7,3},{8,12},{9,13},{10,... | collective-permute-start | bytes 221192 | tf_op jit(solution)/shard_map/ppermute | solution.py:159
  16.7 3.1 %collective-permute-start.13 = (bf16[288,384]{1,0:T(8,128)(2,1)S(1)}, bf16[288,384]{1,0:T(8,128)(2,1)S(1)}, u32[]{:S(2)}, u32[]{:S(2)}) collective-permute-start(bf16[288,384]{1,0:T(8,128)(2,1)S(1)} %pad_maximum_fusion.1), channel_id=1, source_target_pairs={{0,4},{1,5},{2,6},{3,7},{4,0},{5,1},{6,2},{7,3},{8,12},{9,13},{10,... | collective-permute-start | bytes 663560 | tf_op jit(solution)/shard_map/ppermute | solution.py:159
  18.5 2.3 %collective-permute-start.8 = (bf16[288,384]{1,0:T(8,128)(2,1)S(1)}, bf16[288,384]{1,0:T(8,128)(2,1)S(1)}, u32[]{:S(2)}, u32[]{:S(2)}) collective-permute-start(bf16[288,384]{1,0:T(8,128)(2,1)S(1)} %pad_maximum_fusion), channel_id=1, source_target_pairs={{0,4},{1,5},{2,6},{3,7},{4,0},{5,1},{6,2},{7,3},{8,12},{9,13},{10,... | collective-permute-start | bytes 663560 | tf_op jit(solution)/shard_map/ppermute | solution.py:159

commit v5 on v4

--- a/solution.py
+++ b/solution.py
@@ -91,8 +91,8 @@
 
 
 def finish(n, kp, rt, *refs):
-    settled, swap, near_i, near_a = refs[: n - 1], refs[n - 1], refs[n], refs[n + 1]
-    ladder, scale, out, lhs, rhs, buffer, done = refs[n + 2 :]
+    settled, swap, near_i, near_a = refs[: n - 1], refs[n - 1 : n + 1], refs[n + 1], refs[n + 2]
+    ladder, scale, out, lhs, rhs, buffer, done = refs[n + 3 :]
     _, core, shift = place()
 
     def gather(h):
@@ -101,7 +101,8 @@
             if j == 0:
                 (i, i_at), (a, a_at) = (near_i, 0), (near_a, 0)
             else:
-                mine, gift = (settled[j - 1], 0), (swap, 2 * kp * (j - 1))
+                mine = (settled[j - 1], 0)
+                gift = (swap[0], 0) if j == 1 else (swap[1], 2 * kp * (j - 2))
                 (i, i_at), (a, a_at) = (gift, mine) if h == 0 else (mine, gift)
             a_at += h * kp
             lhs[here, :] = a[a_at : a_at + kp, :]
@@ -200,13 +201,14 @@
             lambda k, h, c: (k ^ j, 0, c) if h == carrier(k ^ c ^ j) else (k, 1, c ^ j),
         )
     near = pick(shift, gathered)
-    far = send(near, other)
+    swap_g = send(jnp.concatenate([*[direct[j] for j in range(1, n)], near]), other)
+    far, swap_d = swap_g[2 * kp * (n - 1) :], swap_g[: 2 * kp * (n - 1)]
     has_a = functools.reduce(
         lambda kept, m: jnp.where(shift == m, core == carrier(m), kept), range(n), first
     )
     near_a, near_i = jnp.where(has_a, near, far), jnp.where(has_a, far, near)
     direct, settled = [[x[j] for j in range(1, n)] for x in (direct, settled)]
-    swap_d, swap_s = send(jnp.concatenate(direct), other), send(jnp.concatenate(settled), other)
+    swap_s = [send(settled[0], other), send(jnp.concatenate(settled[1:]), other)]
     early = call(
         functools.partial(prepare, n, kp, rt),
         [*direct, swap_d, energies.reshape(1, -1)],
@@ -217,7 +219,7 @@
     )
     return call(
         functools.partial(finish, n, kp, rt),
-        [*settled, swap_s, near_i, near_a],
+        [*settled, *swap_s, near_i, near_a],
         early,
         pl.BlockSpec(memory_space=pl.ANY),
         jax.ShapeDtypeStruct((rt, 2 * rt), jnp.float32),

time: 22.5 us -> 25.7 us (1.14)
  starting transfers between devices: 14.8 us -> 17 us
  waiting for transfers between devices: 4.61 us -> 5.68 us
    ppermute x14, starting transfers between devices: 14.8 us -> 17 us  [send(): return lax.ppermute(value, AXES, pairs)]
    ppermute x14, waiting for transfers between devices: 4.61 us -> 5.68 us  [send(): return lax.ppermute(value, AXES, pairs)]
  transfers between devices with their start and end apart: 14 -> 14, of which waited for: 7 -> 8; matrix products, arithmetic and copies ran while one was open for 1% -> 0% of each run, Pallas kernels for 6% -> 5%
where the time goes in v5:
time: 25.7 us; the launch traced here: 25.6 us
  starting transfers between devices  17 us (66%)
  waiting for transfers between devices  5.68 us (22%)
  Pallas kernels  2.63 us (10%)
    ppermute x14, starting transfers between devices, send(): return lax.ppermute(value, AXES, pairs)  17 us
    ppermute x14, waiting for transfers between devices, send(): return lax.ppermute(value, AXES, pairs)  5.68 us
    pallas_call x3, Pallas kernels, call(): pl.pallas_call(kernel, in_specs=[keep] * (len(inputs) + len(placed)), out...  1.83 us
    pallas_call x1, Pallas kernels, paired(): pl.pallas_call(load, in_specs=[pl.BlockSpec(memory_space=pltpu.HBM)] * 2,...  0.8 us
  transfers between devices with their start and end apart: 14, of which 8 were waited for; matrix products, arithmetic and copies ran while one was open for 0% of the time, Pallas kernels for 5%

profile of v5, /device:TPU:0, one launch (start us, length us, event | category | flops | bytes accessed | tf_op | source)
XLA Modules:
  0.0 25.6 jit_solution(11643318114439995830)
XLA Ops:
  0.0 0.5 %collective-permute-start = (bf16[48,384]{1,0:T(8,128)(2,1)}, bf16[48,384]{1,0:T(8,128)(2,1)S(1)}, u32[]{:S(2)}, u32[]{:S(2)}) collective-permute-start(bf16[48,384]{1,0:T(8,128)(2,1)} %bitcast.3), channel_id=1, source_target_pairs={{0,4},{1,5},{2,6},{3,7},{4,0},{5,1},{6,2},{7,3},{8,12},{9,13},{10,... | collective-permute-start | bytes 110600 | tf_op jit(solution)/shard_map/ppermute | solution.py:160
  0.5 0.0 collective-permute-start.1
  0.5 0.8 %load.1 = (bf16[48,384]{1,0:T(8,128)(2,1)S(1)}, bf16[24,768]{1,0:T(8,128)(2,1)S(1)}) custom-call(bf16[48,384]{1,0:T(8,128)(2,1)} %bitcast.4, bf16[24,768]{1,0:T(8,128)(2,1)} %refs_1_.1), custom_call_target="tpu_custom_call" | custom-call | tf_op jit(solution)/shard_map/load/pallas_call | solution.py:171
  1.3 0.2 collective-permute-done.their_i
  1.6 0.3 %collective-permute-done.1.their_a = bf16[24,768]{1,0:T(8,128)(2,1)S(1)} collective-permute-done((bf16[24,768]{1,0:T(8,128)(2,1)}, bf16[24,768]{1,0:T(8,128)(2,1)S(1)}, u32[]{:S(2)}, u32[]{:S(2)}) %collective-permute-start.1) | collective-permute-done | bytes 36896 | tf_op jit(solution)/shard_map/ppermute | solution.py:160
  2.0 2.7 %collective-permute-start.3 = (bf16[96,384]{1,0:T(8,128)(2,1)S(1)}, bf16[96,384]{1,0:T(8,128)(2,1)S(1)}, u32[]{:S(2)}, u32[]{:S(2)}) collective-permute-start(bf16[96,384]{1,0:T(8,128)(2,1)S(1)} %get-tuple-element.14.refs_6_), channel_id=1, source_target_pairs={{0,16},{1,17},{2,18},{3,19},{4,6},{5,7},{6,4},{7,5},{8,24},{9,25},... | collective-permute-start | bytes 221192 | tf_op jit(solution)/shard_map/ppermute | solution.py:160
  4.7 1.6 %collective-permute-start.4 = (bf16[96,384]{1,0:T(8,128)(2,1)S(1)}, bf16[96,384]{1,0:T(8,128)(2,1)S(1)}, u32[]{:S(2)}, u32[]{:S(2)}) collective-permute-start(bf16[96,384]{1,0:T(8,128)(2,1)S(1)} %get-tuple-element.13.refs_5_), channel_id=1, source_target_pairs={{0,1},{1,0},{2,3},{3,2},{4,12},{5,13},{6,14},{7,15},{8,9},{9,8},{1... | collective-permute-start | bytes 221192 | tf_op jit(solution)/shard_map/ppermute | solution.py:160
  6.3 2.5 %collective-permute-start.2 = (bf16[96,384]{1,0:T(8,128)(2,1)S(1)}, bf16[96,384]{1,0:T(8,128)(2,1)S(1)}, u32[]{:S(2)}, u32[]{:S(2)}) collective-permute-start(bf16[96,384]{1,0:T(8,128)(2,1)S(1)} %get-tuple-element.13.refs_5_), channel_id=1, source_target_pairs={{0,3},{1,2},{2,1},{3,0},{4,28},{5,29},{6,30},{7,31},{8,11},{9,10},... | collective-permute-start | bytes 221192 | tf_op jit(solution)/shard_map/ppermute | solution.py:160
  8.7 1.4 %collective-permute-start.12 = (bf16[96,384]{1,0:T(8,128)(2,1)S(1)}, bf16[96,384]{1,0:T(8,128)(2,1)S(1)}, u32[]{:S(2)}, u32[]{:S(2)}) collective-permute-start(bf16[96,384]{1,0:T(8,128)(2,1)S(1)} %get-tuple-element.13.refs_5_), channel_id=1, source_target_pairs={{0,24},{1,25},{2,26},{3,27},{4,7},{5,6},{6,5},{7,4},{8,16},{9,17},... | collective-permute-start | bytes 221192 | tf_op jit(solution)/shard_map/ppermute | solution.py:160
  10.2 0.5 %collective-permute-start.10 = (bf16[96,384]{1,0:T(8,128)(2,1)S(1)}, bf16[96,384]{1,0:T(8,128)(2,1)S(1)}, u32[]{:S(2)}, u32[]{:S(2)}) collective-permute-start(bf16[96,384]{1,0:T(8,128)(2,1)S(1)} %get-tuple-element.13.refs_5_), channel_id=1, source_target_pairs={{0,8},{1,9},{2,10},{3,11},{4,5},{5,4},{6,7},{7,6},{8,0},{9,1},{10,... | collective-permute-start | bytes 221192 | tf_op jit(solution)/shard_map/ppermute | solution.py:160
  10.7 1.7 %collective-permute-done.2 = bf16[96,384]{1,0:T(8,128)(2,1)S(1)} collective-permute-done((bf16[96,384]{1,0:T(8,128)(2,1)S(1)}, bf16[96,384]{1,0:T(8,128)(2,1)S(1)}, u32[]{:S(2)}, u32[]{:S(2)}) %collective-permute-start.2) | collective-permute-done | bytes 73760 | tf_op jit(solution)/shard_map/ppermute | solution.py:160
  12.4 0.1 select_select_fusion
  12.5 1.5 %collective-permute-done.12.refs_2_ = bf16[96,384]{1,0:T(8,128)(2,1)S(1)} collective-permute-done((bf16[96,384]{1,0:T(8,128)(2,1)S(1)}, bf16[96,384]{1,0:T(8,128)(2,1)S(1)}, u32[]{:S(2)}, u32[]{:S(2)}) %collective-permute-start.12) | collective-permute-done | bytes 73760 | tf_op jit(solution)/shard_map/ppermute | solution.py:160
  14.0 0.5 %collective-permute-done.10.refs_0_ = bf16[96,384]{1,0:T(8,128)(2,1)S(1)} collective-permute-done((bf16[96,384]{1,0:T(8,128)(2,1)S(1)}, bf16[96,384]{1,0:T(8,128)(2,1)S(1)}, u32[]{:S(2)}, u32[]{:S(2)}) %collective-permute-start.10) | collective-permute-done | bytes 73760 | tf_op jit(solution)/shard_map/ppermute | solution.py:160
  14.6 0.9 %collective-permute-start.13 = (bf16[384,384]{1,0:T(8,128)(2,1)S(1)}, bf16[384,384]{1,0:T(8,128)(2,1)S(1)}, u32[]{:S(2)}, u32[]{:S(2)}) collective-permute-start(bf16[384,384]{1,0:T(8,128)(2,1)S(1)} %pad_maximum_fusion), channel_id=1, source_target_pairs={{0,4},{1,5},{2,6},{3,7},{4,0},{5,1},{6,2},{7,3},{8,12},{9,13},{10,... | collective-permute-start | bytes 884744 | tf_op jit(solution)/shard_map/ppermute | solution.py:160
  15.5 1.5 %collective-permute-start.7 = (bf16[96,384]{1,0:T(8,128)(2,1)S(1)}, bf16[96,384]{1,0:T(8,128)(2,1)S(1)}, u32[]{:S(2)}, u32[]{:S(2)}) collective-permute-start(bf16[96,384]{1,0:T(8,128)(2,1)S(1)} %get-tuple-element.20), channel_id=1, source_target_pairs={{0,24},{1,6},{2,26},{3,4},{4,7},{5,25},{6,5},{7,27},{8,15},{9,17},... | collective-permute-start | bytes 221192 | tf_op jit(solution)/shard_map/ppermute | solution.py:160
  17.0 3.1 %collective-permute-start.5 = (bf16[96,384]{1,0:T(8,128)(2,1)S(1)}, bf16[96,384]{1,0:T(8,128)(2,1)S(1)}, u32[]{:S(2)}, u32[]{:S(2)}) collective-permute-start(bf16[96,384]{1,0:T(8,128)(2,1)S(1)} %get-tuple-element.22), channel_id=1, source_target_pairs={{0,8},{1,4},{2,10},{3,6},{4,5},{5,9},{6,7},{7,11},{8,13},{9,1},{10... | collective-permute-start | bytes 221192 | tf_op jit(solution)/shard_map/ppermute | solution.py:160
  20.1 0.1 collective-permute-done.7.refs_2_
  20.2 0.9 %collective-permute-done.6.refs_1_ = bf16[96,384]{1,0:T(8,128)(2,1)S(1)} collective-permute-done((bf16[96,384]{1,0:T(8,128)(2,1)S(1)}, bf16[96,384]{1,0:T(8,128)(2,1)S(1)}, u32[]{:S(2)}, u32[]{:S(2)}) %collective-permute-start.6) | collective-permute-done | bytes 73760 | tf_op jit(solution)/shard_map/ppermute | solution.py:160
  21.1 1.8 %collective-permute-start.9 = (bf16[192,384]{1,0:T(8,128)(2,1)S(1)}, bf16[192,384]{1,0:T(8,128)(2,1)S(1)}, u32[]{:S(2)}, u32[]{:S(2)}) collective-permute-start(bf16[192,384]{1,0:T(8,128)(2,1)S(1)} %pad_maximum_fusion.1), channel_id=1, source_target_pairs={{0,4},{1,5},{2,6},{3,7},{4,0},{5,1},{6,2},{7,3},{8,12},{9,13},{10,... | collective-permute-start | bytes 442376 | tf_op jit(solution)/shard_map/ppermute | solution.py:160
  22.9 0.5 %collective-permute-start.8 = (bf16[96,384]{1,0:T(8,128)(2,1)S(1)}, bf16[96,384]{1,0:T(8,128)(2,1)S(1)}, u32[]{:S(2)}, u32[]{:S(2)}) collective-permute-start(bf16[96,384]{1,0:T(8,128)(2,1)S(1)} %collective-permute-done.5.refs_0_), channel_id=1, source_target_pairs={{0,4},{1,5},{2,6},{3,7},{4,0},{5,1},{6,2},{7,3},{8,12},{9,13},{10,... | collective-permute-start | bytes 221192 | tf_op jit(solution)/shard_map/ppermute | solution.py:160
  23.4 0.5 %shard_map.38 = (f32[384,768]{1,0:T(8,128)S(1)}, f32[384,768]{1,0:T(8,128)S(1)}) custom-call(bf16[96,384]{1,0:T(8,128)(2,1)S(1)} %collective-permute-done.10.refs_0_, bf16[96,384]{1,0:T(8,128)(2,1)S(1)} %collective-permute-done.11.refs_1_, bf16[96,384]{1,0:T(8,128)(2,1)S(1)} %collective-permute-done.12.refs_2_, bf16[288,384]{1,0:T(8,128)(2,1)S(1)} %slice.9.refs_3_, ...), custom_call_target="tpu_custom_call" | custom-call | tf_op jit(solution)/shard_map/pallas_call | solution.py:135
  23.9 0.4 %collective-permute-done.8.refs_3_ = bf16[96,384]{1,0:T(8,128)(2,1)S(1)} collective-permute-done((bf16[96,384]{1,0:T(8,128)(2,1)S(1)}, bf16[96,384]{1,0:T(8,128)(2,1)S(1)}, u32[]{:S(2)}, u32[]{:S(2)}) %collective-permute-start.8) | collective-permute-done | bytes 73760 | tf_op jit(solution)/shard_map/ppermute | solution.py:160
  24.2 1.3 %shard_map.39 = f32[384,768]{1,0:T(8,128)} custom-call(bf16[96,384]{1,0:T(8,128)(2,1)S(1)} %collective-permute-done.5.refs_0_, bf16[96,384]{1,0:T(8,128)(2,1)S(1)} %collective-permute-done.6.refs_1_, bf16[96,384]{1,0:T(8,128)(2,1)S(1)} %collective-permute-done.7.refs_2_, bf16[96,384]{1,0:T(8,128)(2,1)S(1)} %collective-permute-done.8.refs_3_, ...), custom_call_target="tpu_custom_call" | custom-call | tf_op jit(solution)/shard_map/pallas_call | solution.py:135
  (15 shorter events, 0.1 us)
Async XLA Ops:
  0.0 1.6 %collective-permute-start = (bf16[48,384]{1,0:T(8,128)(2,1)}, bf16[48,384]{1,0:T(8,128)(2,1)S(1)}, u32[]{:S(2)}, u32[]{:S(2)}) collective-permute-start(bf16[48,384]{1,0:T(8,128)(2,1)} %bitcast.3), channel_id=1, source_target_pairs={{0,4},{1,5},{2,6},{3,7},{4,0},{5,1},{6,2},{7,3},{8,12},{9,13},{10,... | collective-permute-start | bytes 110600 | tf_op jit(solution)/shard_map/ppermute | solution.py:160
  0.5 1.4 %collective-permute-start.1 = (bf16[24,768]{1,0:T(8,128)(2,1)}, bf16[24,768]{1,0:T(8,128)(2,1)S(1)}, u32[]{:S(2)}, u32[]{:S(2)}) collective-permute-start(bf16[24,768]{1,0:T(8,128)(2,1)} %refs_1_.1), channel_id=1, source_target_pairs={{0,4},{1,5},{2,6},{3,7},{4,0},{5,1},{6,2},{7,3},{8,12},{9,13},{10,... | collective-permute-start | bytes 110600 | tf_op jit(solution)/shard_map/ppermute | solution.py:160
  1.9 21.4 %copy-start = (f32[3072]{0:T(1024)S(1)}, f32[3072]{0:T(1024)}, u32[]{:S(2)}) copy-start(f32[3072]{0:T(1024)} %param.5) | copy-start | bytes 36868
  2.0 8.2 %collective-permute-start.3 = (bf16[96,384]{1,0:T(8,128)(2,1)S(1)}, bf16[96,384]{1,0:T(8,128)(2,1)S(1)}, u32[]{:S(2)}, u32[]{:S(2)}) collective-permute-start(bf16[96,384]{1,0:T(8,128)(2,1)S(1)} %get-tuple-element.14.refs_6_), channel_id=1, source_target_pairs={{0,16},{1,17},{2,18},{3,19},{4,6},{5,7},{6,4},{7,5},{8,24},{9,25},... | collective-permute-start | bytes 221192 | tf_op jit(solution)/shard_map/ppermute | solution.py:160
  4.7 6.0 %collective-permute-start.4 = (bf16[96,384]{1,0:T(8,128)(2,1)S(1)}, bf16[96,384]{1,0:T(8,128)(2,1)S(1)}, u32[]{:S(2)}, u32[]{:S(2)}) collective-permute-start(bf16[96,384]{1,0:T(8,128)(2,1)S(1)} %get-tuple-element.13.refs_5_), channel_id=1, source_target_pairs={{0,1},{1,0},{2,3},{3,2},{4,12},{5,13},{6,14},{7,15},{8,9},{9,8},{1... | collective-permute-start | bytes 221192 | tf_op jit(solution)/shard_map/ppermute | solution.py:160
  6.3 6.2 %collective-permute-start.2 = (bf16[96,384]{1,0:T(8,128)(2,1)S(1)}, bf16[96,384]{1,0:T(8,128)(2,1)S(1)}, u32[]{:S(2)}, u32[]{:S(2)}) collective-permute-start(bf16[96,384]{1,0:T(8,128)(2,1)S(1)} %get-tuple-element.13.refs_5_), channel_id=1, source_target_pairs={{0,3},{1,2},{2,1},{3,0},{4,28},{5,29},{6,30},{7,31},{8,11},{9,10},... | collective-permute-start | bytes 221192 | tf_op jit(solution)/shard_map/ppermute | solution.py:160
  8.7 3.8 %collective-permute-start.11 = (bf16[96,384]{1,0:T(8,128)(2,1)S(1)}, bf16[96,384]{1,0:T(8,128)(2,1)S(1)}, u32[]{:S(2)}, u32[]{:S(2)}) collective-permute-start(bf16[96,384]{1,0:T(8,128)(2,1)S(1)} %get-tuple-element.14.refs_6_), channel_id=1, source_target_pairs={{0,6},{1,7},{2,4},{3,5},{4,16},{5,17},{6,18},{7,19},{8,14},{9,15},... | collective-permute-start | bytes 221192 | tf_op jit(solution)/shard_map/ppermute | solution.py:160
  8.7 5.3 %collective-permute-start.12 = (bf16[96,384]{1,0:T(8,128)(2,1)S(1)}, bf16[96,384]{1,0:T(8,128)(2,1)S(1)}, u32[]{:S(2)}, u32[]{:S(2)}) collective-permute-start(bf16[96,384]{1,0:T(8,128)(2,1)S(1)} %get-tuple-element.13.refs_5_), channel_id=1, source_target_pairs={{0,24},{1,25},{2,26},{3,27},{4,7},{5,6},{6,5},{7,4},{8,16},{9,17},... | collective-permute-start | bytes 221192 | tf_op jit(solution)/shard_map/ppermute | solution.py:160
  10.2 4.4 %collective-permute-start.10 = (bf16[96,384]{1,0:T(8,128)(2,1)S(1)}, bf16[96,384]{1,0:T(8,128)(2,1)S(1)}, u32[]{:S(2)}, u32[]{:S(2)}) collective-permute-start(bf16[96,384]{1,0:T(8,128)(2,1)S(1)} %get-tuple-element.13.refs_5_), channel_id=1, source_target_pairs={{0,8},{1,9},{2,10},{3,11},{4,5},{5,4},{6,7},{7,6},{8,0},{9,1},{10,... | collective-permute-start | bytes 221192 | tf_op jit(solution)/shard_map/ppermute | solution.py:160
  14.6 8.8 %collective-permute-start.13 = (bf16[384,384]{1,0:T(8,128)(2,1)S(1)}, bf16[384,384]{1,0:T(8,128)(2,1)S(1)}, u32[]{:S(2)}, u32[]{:S(2)}) collective-permute-start(bf16[384,384]{1,0:T(8,128)(2,1)S(1)} %pad_maximum_fusion), channel_id=1, source_target_pairs={{0,4},{1,5},{2,6},{3,7},{4,0},{5,1},{6,2},{7,3},{8,12},{9,13},{10,... | collective-permute-start | bytes 884744 | tf_op jit(solution)/shard_map/ppermute | solution.py:160
  15.5 4.7 %collective-permute-start.7 = (bf16[96,384]{1,0:T(8,128)(2,1)S(1)}, bf16[96,384]{1,0:T(8,128)(2,1)S(1)}, u32[]{:S(2)}, u32[]{:S(2)}) collective-permute-start(bf16[96,384]{1,0:T(8,128)(2,1)S(1)} %get-tuple-element.20), channel_id=1, source_target_pairs={{0,24},{1,6},{2,26},{3,4},{4,7},{5,25},{6,5},{7,27},{8,15},{9,17},... | collective-permute-start | bytes 221192 | tf_op jit(solution)/shard_map/ppermute | solution.py:160
  17.0 4.1 %collective-permute-start.6 = (bf16[96,384]{1,0:T(8,128)(2,1)S(1)}, bf16[96,384]{1,0:T(8,128)(2,1)S(1)}, u32[]{:S(2)}, u32[]{:S(2)}) collective-permute-start(bf16[96,384]{1,0:T(8,128)(2,1)S(1)} %get-tuple-element.21), channel_id=1, source_target_pairs={{0,6},{1,17},{2,4},{3,19},{4,16},{5,7},{6,18},{7,5},{8,24},{9,15},... | collective-permute-start | bytes 221192 | tf_op jit(solution)/shard_map/ppermute | solution.py:160
  17.0 5.9 %collective-permute-start.5 = (bf16[96,384]{1,0:T(8,128)(2,1)S(1)}, bf16[96,384]{1,0:T(8,128)(2,1)S(1)}, u32[]{:S(2)}, u32[]{:S(2)}) collective-permute-start(bf16[96,384]{1,0:T(8,128)(2,1)S(1)} %get-tuple-element.22), channel_id=1, source_target_pairs={{0,8},{1,4},{2,10},{3,6},{4,5},{5,9},{6,7},{7,11},{8,13},{9,1},{10... | collective-permute-start | bytes 221192 | tf_op jit(solution)/shard_map/ppermute | solution.py:160
  21.1 3.1 %collective-permute-start.9 = (bf16[192,384]{1,0:T(8,128)(2,1)S(1)}, bf16[192,384]{1,0:T(8,128)(2,1)S(1)}, u32[]{:S(2)}, u32[]{:S(2)}) collective-permute-start(bf16[192,384]{1,0:T(8,128)(2,1)S(1)} %pad_maximum_fusion.1), channel_id=1, source_target_pairs={{0,4},{1,5},{2,6},{3,7},{4,0},{5,1},{6,2},{7,3},{8,12},{9,13},{10,... | collective-permute-start | bytes 442376 | tf_op jit(solution)/shard_map/ppermute | solution.py:160
  22.9 1.4 %collective-permute-start.8 = (bf16[96,384]{1,0:T(8,128)(2,1)S(1)}, bf16[96,384]{1,0:T(8,128)(2,1)S(1)}, u32[]{:S(2)}, u32[]{:S(2)}) collective-permute-start(bf16[96,384]{1,0:T(8,128)(2,1)S(1)} %collective-permute-done.5.refs_0_), channel_id=1, source_target_pairs={{0,4},{1,5},{2,6},{3,7},{4,0},{5,1},{6,2},{7,3},{8,12},{9,13},{10,... | collective-permute-start | bytes 221192 | tf_op jit(solution)/shard_map/ppermute | solution.py:160
